TPU v7x, 128 devices: a whole 4x4x4 slice. The times are simulated.
128 devices in a mesh: tile: 16 (over z, x), seq: 8 (over y, core).
Axes of the slice: x: 4, y: 4, z: 4, core: 2. Of those that a mesh axis runs over, the one named last changes fastest.
Arguments:
- pixels: bfloat16 [8192, 128, 384], P(('tile', 'seq')), may hold values from -6 to 6
- encoder_ids: int32 [8192, 1], P(('tile', 'seq')), may hold values from 0 to 15; in each aligned block of 64 rows (0 to 63, 64 to 127, ...) at most 8 rows name the same one
- stem_weight: bfloat16 [4, 4, 3, 64], replicated, may hold values from -1.25 to 1.25
- conv_weight: bfloat16 [3, 3, 64, 128], replicated, may hold values from -0.375 to 0.375
- point_weight: bfloat16 [128, 256], replicated, may hold values from -0.75 to 0.75
- proj_weight: bfloat16 [256, 768], replicated, may hold values from -0.5 to 0.5
- qkv_weight: bfloat16 [768, 2304], replicated, may hold values from -2 to 2
- out_weight: bfloat16 [768, 768], replicated, may hold values from -0.4375 to 0.4375
Outputs:
- slide_out: bfloat16 [16, 1024, 768], P('tile', 'seq')
Inputs may be any that keep to these rules, and one draw needn't show every extreme that they name: `encoder_ids`: among the 64 tiles of one reader device at most 8 name the same encoder, and in some devices one encoder is named exactly 8 times.
All inputs are finite; a program needn't handle non-finite values.
Results may differ from a plain program's by a relative error of at most 0.02.
Values may be sent and summed in bfloat16 or wider, within the bound.
A program may use at most 128 MiB of HBM per device.

v0:
```python
import jax
import jax.numpy as jnp
from jax import lax
from jax.sharding import PartitionSpec as P

D = 768
ATTENTION_HEADS = 12
HEAD_SIZE = 64


def conv_stack(tiles, stem_weight, conv_weight, point_weight, proj_weight):
    tile_count = tiles.shape[0]
    tile_side = tiles.shape[1]
    picture = tiles.reshape(tile_count, tile_side, tile_side, 3)
    layout_spec = ("NHWC", "HWIO", "NHWC")
    stem_out = lax.conv_general_dilated(
        picture,
        stem_weight,
        (4, 4),
        "VALID",
        dimension_numbers=layout_spec,
        preferred_element_type=jnp.float32,
    )
    stem_out = jax.nn.relu(stem_out).astype(jnp.bfloat16)
    middle = lax.conv_general_dilated(
        stem_out,
        conv_weight,
        (2, 2),
        ((1, 1), (1, 1)),
        dimension_numbers=layout_spec,
        preferred_element_type=jnp.float32,
    )
    middle = jax.nn.relu(middle).astype(jnp.bfloat16)
    point_out = jnp.einsum(
        "nhwc,cd->nhwd", middle[:, ::2, ::2, :], point_weight, preferred_element_type=jnp.float32
    )
    pooled = jnp.mean(jax.nn.relu(point_out), axis=(1, 2)).astype(jnp.bfloat16)
    return jnp.dot(pooled, proj_weight, preferred_element_type=jnp.float32).astype(jnp.bfloat16)


def slide_layer(rows, live, qkv_weight, out_weight):
    sequence_count = lax.axis_size("seq")
    seg_len = rows.shape[0]
    dilation_groups = seg_len // sequence_count
    wide = rows.astype(jnp.float32)
    power = jnp.mean(wide * wide, axis=-1, keepdims=True)
    normed = (wide * lax.rsqrt(power + 1e-06)).astype(jnp.bfloat16)
    packed = jnp.dot(normed, qkv_weight, preferred_element_type=jnp.float32)
    query_rows = (
        packed[:, :D]
        .astype(jnp.bfloat16)
        .astype(jnp.float32)
        .reshape(seg_len, ATTENTION_HEADS, HEAD_SIZE)
    )
    keys_bf = packed[:, D : 2 * D].astype(jnp.bfloat16)
    values_bf = packed[:, 2 * D :].astype(jnp.bfloat16)
    key_rows = keys_bf.astype(jnp.float32).reshape(seg_len, ATTENTION_HEADS, HEAD_SIZE)
    value_rows = values_bf.astype(jnp.float32).reshape(seg_len, ATTENTION_HEADS, HEAD_SIZE)
    score_scale = 1.0 / jnp.sqrt(jnp.float32(HEAD_SIZE))
    scores = jnp.einsum("phd,qhd->hpq", query_rows, key_rows) * score_scale
    places = jnp.arange(seg_len)
    alive = live > 0.5
    local = alive[None, :] | (places[:, None] == places[None, :])
    masked = jnp.where(local[None], scores, jnp.float32(-1e30))
    top_local = jnp.max(masked, axis=-1)
    weights = jnp.exp(masked - top_local[:, :, None]) * local[None].astype(jnp.float32)
    den_local = jnp.sum(weights, axis=-1)
    local_accumulator = jnp.einsum("hpq,qhd->hpd", weights, value_rows)
    offsets = jnp.arange(ATTENTION_HEADS) % sequence_count
    dilation_selector = (jnp.arange(sequence_count)[:, None] == offsets[None, :]).astype(
        jnp.float32
    )
    selected_query = jnp.einsum(
        "bnpo,np->pbo",
        query_rows.reshape(dilation_groups, sequence_count, ATTENTION_HEADS, HEAD_SIZE),
        dilation_selector,
    )
    selected_keys = jnp.einsum(
        "bnpo,np->pbo",
        key_rows.reshape(dilation_groups, sequence_count, ATTENTION_HEADS, HEAD_SIZE),
        dilation_selector,
    ).astype(jnp.bfloat16)
    values_sel = jnp.einsum(
        "bnpo,np->pbo",
        value_rows.reshape(dilation_groups, sequence_count, ATTENTION_HEADS, HEAD_SIZE),
        dilation_selector,
    ).astype(jnp.bfloat16)
    live_sel = jnp.einsum(
        "mr,rh->hm", live.reshape(dilation_groups, sequence_count), dilation_selector
    ).astype(jnp.bfloat16)
    start_top = jnp.einsum(
        "hmr,rh->hm",
        top_local.reshape(ATTENTION_HEADS, dilation_groups, sequence_count),
        dilation_selector,
    )
    start_den = jnp.einsum(
        "hmr,rh->hm",
        den_local.reshape(ATTENTION_HEADS, dilation_groups, sequence_count),
        dilation_selector,
    )
    initial_accumulator = jnp.einsum(
        "bstc,tb->bsc",
        local_accumulator.reshape(ATTENTION_HEADS, dilation_groups, sequence_count, HEAD_SIZE),
        dilation_selector,
    )
    segment_keys = lax.all_gather(selected_keys, "seq", axis=1, tiled=True)
    segment_values = lax.all_gather(values_sel, "seq", axis=1, tiled=True)
    piece_live = lax.all_gather(live_sel, "seq", axis=1, tiled=True)
    usable = piece_live.astype(jnp.float32) > 0.5
    partial_scores = (
        jnp.einsum("psi,pei->pse", selected_query, segment_keys.astype(jnp.float32)) * score_scale
    )
    part_masked = jnp.where(usable[:, None, :], partial_scores, jnp.float32(-1e30))
    new_top = jnp.maximum(start_top, jnp.max(part_masked, axis=-1))
    rescale = jnp.exp(start_top - new_top)
    partial_weights = jnp.exp(part_masked - new_top[:, :, None]) * usable[:, None, :].astype(
        jnp.float32
    )
    new_den = start_den * rescale + jnp.sum(partial_weights, axis=-1)
    new_acc = initial_accumulator * rescale[:, :, None] + jnp.einsum(
        "zfj,zjg->zfg", partial_weights, segment_values.astype(jnp.float32)
    )
    context_sel = new_acc / new_den[:, :, None]
    context_local = (local_accumulator / den_local[:, :, None]).reshape(
        ATTENTION_HEADS, dilation_groups, sequence_count, HEAD_SIZE
    )
    choose = jnp.transpose(dilation_selector, (1, 0))[:, None, :, None]
    context = context_local * (1.0 - choose) + context_sel[:, :, None, :] * choose
    context = (
        jnp.transpose(context.reshape(ATTENTION_HEADS, seg_len, HEAD_SIZE), (1, 0, 2))
        .reshape(seg_len, D)
        .astype(jnp.bfloat16)
    )
    result = jnp.dot(context, out_weight, preferred_element_type=jnp.float32) * live[:, None]
    return result.astype(jnp.bfloat16)


def body(
    pixels, encoder_ids, stem_weight, conv_weight, point_weight, proj_weight, qkv_weight, out_weight
):
    n_tile = lax.axis_size("tile")
    tok_here = pixels.shape[0]
    capacity = 2 * tok_here // n_tile
    targets = encoder_ids[:, 0]
    order = jnp.arange(tok_here, dtype=jnp.int32)
    same = (targets[:, None] == targets[None, :]) & (order[None, :] < order[:, None])
    ranks = jnp.sum(same.astype(jnp.int32), axis=1)
    slots = targets * capacity + ranks
    flags = (
        jnp.zeros((n_tile * capacity,), jnp.bfloat16)
        .at[slots]
        .set(jnp.bfloat16(1.0))
        .reshape(n_tile, capacity)
    )
    buffer = jnp.zeros((n_tile * capacity,) + pixels.shape[1:], jnp.bfloat16).at[slots].set(pixels)
    buffer = buffer.reshape((n_tile, capacity) + pixels.shape[1:])
    piece_pixels = lax.all_to_all(buffer, "tile", split_axis=0, concat_axis=0, tiled=True)
    piece_flags = lax.all_to_all(flags, "tile", split_axis=0, concat_axis=0, tiled=True)
    flat = piece_pixels.reshape((-1,) + piece_pixels.shape[2:])
    embeds = conv_stack(flat, stem_weight, conv_weight, point_weight, proj_weight)
    arrived = embeds.reshape(piece_pixels.shape[0], piece_pixels.shape[1], -1)
    rows = arrived.reshape(n_tile * capacity, -1)
    live = piece_flags.reshape(-1).astype(jnp.float32)
    return slide_layer(rows, live, qkv_weight, out_weight)[None]


def solution(mesh):
    return jax.shard_map(
        body,
        mesh=mesh,
        in_specs=(
            P(("tile", "seq"), None, None),
            P(("tile", "seq"), None),
            P(),
            P(),
            P(),
            P(),
            P(),
            P(),
        ),
        out_specs=P("tile", "seq", None),
        check_vma=False,
    )
```

profile of v0, /device:TPU:1, one launch (start us, length us, event | category | flops | bytes accessed | tf_op | source)
XLA Modules:
  0.0 380.3 jit_solution(15095297947952436610)
XLA Ops:
  0.0 1.0 convert_reduce_fusion
  1.0 0.8 fusion.41
  1.8 1.0 scatter_custom_fusion
  3.4 8.4 %all-to-all-start = ((bf16[16,1,8]{2,1,0:T(2,128)(2,1)}), bf16[16,1,8]{2,1,0:T(2,128)(2,1)S(1)}, u32[]{:S(2)}, u32[]{:S(2)}) async-start(bf16[16,1,8]{2,1,0:T(2,128)(2,1)} %all_to_all.15), calls=%async_computation | async-start | bytes 16384 | tf_op jit(solution)/shard_map/all_to_all | solution.py:158
  11.8 6.6 %broadcast_in_dim.35 = bf16[128,128,384]{2,1,0:T(8,128)(2,1)} broadcast(bf16[]{:T(256)} %constant.15.clone.1), dimensions={} | broadcast | bytes 12582914 | tf_op jit(solution)/shard_map/broadcast_in_dim | solution.py:155
  18.4 20.1 %scatter_fusion = bf16[128,128,384]{2,1,0:T(8,128)(2,1)} fusion(bf16[128,128,384]{2,1,0:T(8,128)(2,1)} %broadcast_in_dim.35, s32[64]{0:T(128)S(1)} %fusion.41, bf16[64,128,384]{2,1,0:T(8,128)(2,1)} %param.8), kind=kCustom, calls=%fused_computation.1 | custom fusion | bytes 18874624 | tf_op jit(solution)/shard_map/scatter | solution.py:155
  38.6 6.8 %all-to-all-start.1 = ((bf16[16,8,128,384]{3,2,1,0:T(8,128)(2,1)}), bf16[16,8,128,384]{3,2,1,0:T(8,128)(2,1)}, u32[]{:S(2)}, u32[]{:S(2)}) async-start(bf16[16,8,128,384]{3,2,1,0:T(8,128)(2,1)} %bitcast.74), calls=%async_computation.1 | async-start | bytes 25165824 | tf_op jit(solution)/shard_map/all_to_all | solution.py:157
  46.0 1.4 copy.72
  48.7 1.6 mul.108
  51.1 1.6 mul.121
  52.7 0.8 convolution_convert_fusion.2
  53.6 15.3 %all_gather.9 = bf16[12,128]{0,1:T(8,128)(2,1)} all-gather(bf16[12,16]{0,1:T(8,128)(2,1)S(1)} %copy.67), channel_id=1, replica_groups=mesh['tile'=16,'seq'=8] {'seq'}, dimensions={1}, use_global_device_ids=true | all-gather | bytes 3456 | tf_op jit(solution)/shard_map/all_gather | solution.py:108
  68.9 1.4 copy.68
  70.5 1.3 fusion.47
  71.8 0.7 fusion.40
  72.5 156.2 %all-to-all-done.1 = bf16[16,8,128,384]{3,2,1,0:T(8,128)(2,1)} async-done(((bf16[16,8,128,384]{3,2,1,0:T(8,128)(2,1)}), bf16[16,8,128,384]{3,2,1,0:T(8,128)(2,1)}, u32[]{:S(2)}, u32[]{:S(2)}) %all-to-all-start.1) | async-done | bytes 12582944 | tf_op jit(solution)/shard_map/all_to_all | solution.py:157
  228.7 16.7 %copy.57 = bf16[16,8,128,384]{2,1,0,3:T(8,128)(2,1)} copy(bf16[16,8,128,384]{3,2,1,0:T(8,128)(2,1)} %all-to-all-done.1) | data formatting | bytes 25165824 | tf_op jit(solution)/shard_map/all_to_all | solution.py:157
  245.4 27.1 %copy.58 = bf16[128,128,128,3]{0,3,2,1:T(4,128)(2,1)} copy(bf16[128,128,128,3]{1,0,3,2:T(8,128)(2,1)} %bitcast.75) | data formatting | bytes 25165824 | tf_op jit(solution)/shard_map/reshape;reshape | solution.py:14
  272.5 30.2 %maximum_convert_fusion.2 = bf16[128,16,16,128]{3,0,2,1:T(8,128)(2,1)} fusion(bf16[3,3,64,128]{3,2,1,0:T(8,128)(2,1)} %param.11, bf16[128,128,128,3]{0,3,2,1:T(4,128)(2,1)} %copy.58, bf16[4,4,3,64]{3,1,2,0:T(4,128)(2,1)S(1)} %copy-done.5), kind=kOutput, calls=%fused_computation.4 | convolution fusion | flops 5463080960 | bytes 21125120 | tf_op jit(solution)/shard_map/conv_general_dilated | solution.py:25
  302.7 1.8 slice.15
  304.5 3.6 maximum_reduce_fusion
  309.1 0.8 fusion.48
  309.9 2.1 reshape_reshape.13
  312.0 1.7 copy.61
  313.7 2.1 reshape_reshape.14
  315.8 1.7 copy.62
  317.6 1.7 copy.63
  319.3 2.1 reshape_reshape.15
  321.4 1.3 fusion.17
  322.7 16.7 %all_gather.10 = bf16[12,128,64]{2,1,0:T(8,128)(2,1)} all-gather(bf16[12,16,64]{2,1,0:T(8,128)(2,1)S(1)} %convert_element_type.105), channel_id=1, replica_groups=mesh['tile'=16,'seq'=8] {'seq'}, dimensions={1}, use_global_device_ids=true | all-gather | bytes 221184 | tf_op jit(solution)/shard_map/all_gather | solution.py:106
  339.4 1.9 fusion.19
  341.3 2.2 fusion.49
  343.5 0.7 reshape.178
  344.3 1.3 fusion.13
  346.3 1.5 fusion.51
  347.8 1.5 fusion.52
  349.3 2.2 fusion.14
  351.6 1.9 copy.65
  353.5 1.2 fusion.11
  354.7 1.3 fusion.15
  356.0 13.0 %all_gather.11 = bf16[12,128,64]{2,1,0:T(8,128)(2,1)S(1)} all-gather(bf16[12,16,64]{2,1,0:T(8,128)(2,1)S(1)} %convert_element_type.107), channel_id=1, replica_groups=mesh['tile'=16,'seq'=8] {'seq'}, dimensions={1}, use_global_device_ids=true | all-gather | bytes 221184 | tf_op jit(solution)/shard_map/all_gather | solution.py:107
  369.0 1.4 fusion.50
  371.1 0.9 fusion.24
  372.7 1.0 fusion.10
  373.7 1.0 broadcast_bitcast_fusion
  374.7 2.1 copy.69
  376.8 1.2 add_convert_fusion
  378.0 2.3 fusion.8
  (35 shorter events, 6.9 us)
Async XLA Ops:
  0.0 308.4 %copy-start = (bf16[768,2304]{1,0:T(8,128)(2,1)S(1)}, bf16[768,2304]{1,0:T(8,128)(2,1)}, u32[]{:S(2)}) copy-start(bf16[768,2304]{1,0:T(8,128)(2,1)} %param.14) | copy-start | bytes 10616836
  3.4 35.1 %all-to-all-start = ((bf16[16,1,8]{2,1,0:T(2,128)(2,1)}), bf16[16,1,8]{2,1,0:T(2,128)(2,1)S(1)}, u32[]{:S(2)}, u32[]{:S(2)}) async-start(bf16[16,1,8]{2,1,0:T(2,128)(2,1)} %all_to_all.15), calls=%async_computation | async-start | bytes 16384 | tf_op jit(solution)/shard_map/all_to_all | solution.py:158
  38.6 190.1 %all-to-all-start.1 = ((bf16[16,8,128,384]{3,2,1,0:T(8,128)(2,1)}), bf16[16,8,128,384]{3,2,1,0:T(8,128)(2,1)}, u32[]{:S(2)}, u32[]{:S(2)}) async-start(bf16[16,8,128,384]{3,2,1,0:T(8,128)(2,1)} %bitcast.74), calls=%async_computation.1 | async-start | bytes 25165824 | tf_op jit(solution)/shard_map/all_to_all | solution.py:157
  45.4 5.7 %copy-start.3 = (s32[12]{0:T(128)}, s32[12]{0:T(128)S(1)}, u32[]{:S(2)}) copy-start(s32[12]{0:T(128)S(1)} %and_select_fusion) | copy-start | bytes 148
  70.5 174.9 %copy-start.4 = (f32[128]{0:T(128)}, f32[128]{0:T(128)S(1)}, u32[]{:S(2)}) copy-start(f32[128]{0:T(128)S(1)} %reshape.180) | copy-start | bytes 1540
  245.4 27.1 %copy-start.5 = (bf16[4,4,3,64]{3,1,2,0:T(4,128)(2,1)S(1)}, bf16[4,4,3,64]{3,1,2,0:T(4,128)(2,1)}, u32[]{:S(2)}) copy-start(bf16[4,4,3,64]{3,1,2,0:T(4,128)(2,1)} %param.10) | copy-start | bytes 18436
  302.7 5.4 %copy-start.1 = (bf16[256,768]{1,0:T(8,128)(2,1)S(1)}, bf16[256,768]{1,0:T(8,128)(2,1)}, u32[]{:S(2)}) copy-start(bf16[256,768]{1,0:T(8,128)(2,1)} %param.13) | copy-start | bytes 1179652
  304.5 16.9 %copy-start.2 = (pred[8,12,1,1]{0,2,3,1:T(4,128)(4,1)S(1)}, pred[8,12,1,1]{0,2,3,1:T(4,128)(4,1)}, u32[]{:S(2)}) copy-start(pred[8,12,1,1]{0,2,3,1:T(4,128)(4,1)} %copy.72) | copy-start | bytes 292
where the time goes:
time: 383 us; the launch traced here: 380 us
  waiting for transfers between devices  156 us (41%)
  local copies, waits for them, and re-layouts  101 us (26%)
  matrix products  53.5 us (14%)
  blocking collectives  45 us (12%)
  starting transfers between devices  15.2 us (4%)
  other arithmetic  9.33 us (2%)
    all_to_all x1, waiting for transfers between devices, body(): lax.all_to_all(buffer, 'tile', split_axis=0, concat_axis=0, tiled=True)  156 us
    conv_general_dilated x1, matrix products, conv_stack(): lax.conv_general_dilated(stem_out, conv_weight, (2, 2), ((1, 1), (1, 1)),...  30.2 us
    another operation x1, local copies, waits for them, and re-layouts, conv_stack(): picture = tiles.reshape(tile_count, tile_side, tile_side, 3)  27.1 us
    scatter x1, local copies, waits for them, and re-layouts, body(): jnp.zeros((n_tile * capacity,) + pixels.shape[1:], jnp.bfloat16).at[slots]  20.1 us
    all_gather x1, blocking collectives, slide_layer(): segment_keys = lax.all_gather(selected_keys, 'seq', axis=1, tiled=True)  16.7 us
    all_to_all x1, local copies, waits for them, and re-layouts, body(): lax.all_to_all(buffer, 'tile', split_axis=0, concat_axis=0, tiled=True)  16.7 us
    all_gather x1, blocking collectives, slide_layer(): piece_live = lax.all_gather(live_sel, 'seq', axis=1, tiled=True)  15.3 us
    all_gather x1, blocking collectives, slide_layer(): segment_values = lax.all_gather(values_sel, 'seq', axis=1, tiled=True)  13 us
  transfers between devices with their start and end apart: 2, of which 1 were waited for; matrix products, arithmetic and copies ran while one was open for 10% of the time, Pallas kernels for 0%

commit v1 on v0

--- a/solution.py
+++ b/solution.py
@@ -1,41 +1,181 @@
+import functools
 import jax
 import jax.numpy as jnp
 from jax import lax
 from jax.sharding import PartitionSpec as P
+from jax.experimental import pallas as pl
+from jax.experimental.pallas import tpu as pltpu
 
 D = 768
+C1, C2, C3 = 64, 128, 256
+GROUP = 16
+LINE = D + 128
+F32, BF16 = jnp.float32, jnp.bfloat16
+
+BLOCKS = (
+    ((0, 0, 1), (1, 0, 2), (3, 1, 0), (4, 1, 1)),
+    ((5, 0, 2), (7, 1, 0), (8, 1, 1), (9, 1, 2)),
+    ((11, 0, 0), (12, 0, 1), (13, 0, 2), (15, 1, 0)),
+)
+
+
+def iota(shape, dim):
+    return lax.broadcasted_iota(jnp.int32, shape, dim)
+
+
+def dot(a, b):
+    return jnp.dot(a, b, preferred_element_type=F32)
+
+
+def stem_spread(stem_ref, flat_ref, base):
+    taps = iota((256, 64), 1)
+    rows = iota((256, 64), 0)
+    lane = (rows & 63) + base
+    lane = lane - 12 * jnp.floor((lane.astype(F32) + 0.5) * (1.0 / 12.0)).astype(jnp.int32)
+    colour, column = (taps & 15) >> 2, taps & 3
+    hit = ((rows >> 6) == (taps >> 4)) & (colour < 3) & (lane == 3 * column + colour)
+    chosen = jnp.where(hit, 1.0, 0.0).astype(BF16)
+    tiled = jnp.where((iota((64, 256), 1) & 63) == iota((64, 256), 0), 1.0, 0.0).astype(BF16)
+    wide = dot(flat_ref[...].astype(BF16), tiled).astype(BF16)
+    return dot(chosen, wide)
+
+
+def stem_block(spread, base, block):
+    lane = (iota((256, 256), 0) & 63) + base
+    quarter = iota((256, 256), 1) >> 6
+    first = jnp.zeros((256, 256), jnp.int32)
+    for q, (column, _, _) in enumerate(block):
+        first = jnp.where(quarter == q, 12 * column, first)
+    return jnp.where((lane >= first) & (lane < first + 12), spread, 0.0).astype(BF16)
+
+
+def encode_kernel(steps, pix_ref, ids_ref, stem_ref, conv_ref, point_ref, proj_ref, out_ref,
+                  flat, stem_w, conv_w, picked, packed, hidden, middle, pooled):
+    step = pl.program_id(0)
+    n_tiles = pix_ref.shape[0] // 128
+    n_blocks = n_tiles // 2
+    n_rows = n_tiles * 8
+
+    @pl.when(step == 0)
+    def _():
+        flat[...] = jnp.zeros_like(flat)
+        for a in range(4):
+            for c in range(3):
+                flat[a * 16 + c * 4:a * 16 + c * 4 + 4, :] = stem_ref[a, c].astype(F32)
+        for base, uses in ((0, ((0, 0), (1, 1))), (64, ((2, 1),)), (128, ((3, 2),))):
+            spread = stem_spread(stem_ref, flat, base)
+            for slot, block in uses:
+                stem_w[slot] = stem_block(spread, base, BLOCKS[block])
+        conv_w[...] = jnp.zeros_like(conv_w)
+        for n, block in enumerate(BLOCKS):
+            for d in range(3):
+                for q, (_, side, tap) in enumerate(block):
+                    row = d * 256 + q * 64
+                    conv_w[n, row:row + 64, side * 128:side * 128 + 128] = conv_ref[d, tap]
+        row, col = iota((192, 256), 0), iota((192, 256), 1)
+        tap_row, g = row >> 4, row & 15
+        a, d = tap_row & 3, tap_row >> 2
+        row_of = 16 * g + 4 * (d - 1) + a
+        good = (row_of == col) & ((d > 0) | ((g & 7) > 0))
+        picked[...] = jnp.where(good, 1.0, 0.0).astype(BF16)
+
+    for b in range(n_blocks):
+        rows = dot(picked[...], pix_ref[b * 256:b * 256 + 256, :]).astype(BF16)
+        for d in range(3):
+            for pair in range(2):
+                first = (d * 4 + pair * 2) * 16
+                p0, p1 = rows[first:first + 16], rows[first + 16:first + 32]
+                for c in range(3):
+                    lo = c * 128
+                    for half in range(2):
+                        unit = 2 * c + half
+                        at = lo + half * 64
+                        h, u = unit // 3, unit % 3
+                        packed[u, (h * 3 + d) * n_rows + b * 16:(h * 3 + d) * n_rows + b * 16 + 16,
+                               pair * 128:pair * 128 + 128] = jnp.concatenate(
+                                   [p0[:, at:at + 64], p1[:, at:at + 64]], axis=1)
+
+    for n, terms in enumerate((((0, 0),), ((0, 1), (1, 2)), ((2, 3),))):
+        total = dot(packed[terms[0][0]], stem_w[terms[0][1]])
+        for u, w in terms[1:]:
+            total = total + dot(packed[u], stem_w[w])
+        total = jnp.maximum(total, 0.0).astype(BF16)
+        for h in range(2):
+            for d in range(3):
+                hidden[n, h * n_rows:(h + 1) * n_rows, d * 256:(d + 1) * 256] = (
+                    total[(h * 3 + d) * n_rows:(h * 3 + d + 1) * n_rows])
+    left = dot(hidden[0], conv_w[0])
+    mid = dot(hidden[1], conv_w[1])
+    right = dot(hidden[2], conv_w[2])
+    for h in range(2):
+        rows = slice(h * n_rows, (h + 1) * n_rows)
+        first = left[rows, :128]
+        if h == 1:
+            first = first + right[:n_rows, 128:]
+        cols = (first, left[rows, 128:] + mid[rows, :128], mid[rows, 128:], right[rows, :128])
+        for j, col in enumerate(cols):
+            at = (h * 4 + j) * n_rows
+            middle[at:at + n_rows, :] = jnp.maximum(col, 0.0).astype(BF16)
+    point = jnp.maximum(dot(middle[...], point_ref[...]), 0.0)
+    summed = point[:n_rows]
+    for j in range(1, 8):
+        summed = summed + point[j * n_rows:(j + 1) * n_rows]
+    mean = jnp.sum(summed.reshape(n_tiles, 8, C3), axis=1) * (1.0 / 64.0)
+    pooled[pl.ds(pl.multiple_of(step * n_tiles, n_tiles), n_tiles), :] = mean.astype(BF16)
+
+    @pl.when(step == steps - 1)
+    def _():
+        embed = dot(pooled[...], proj_ref[...]).astype(BF16)
+        n = embed.shape[0]
+        across = jnp.broadcast_to(ids_ref[...], (n, n))
+        own = iota((n, n), 0) == iota((n, n), 1)
+        down = jnp.sum(jnp.where(own, across, 0), axis=1, keepdims=True)
+        same = (down == across) & (iota((n, n), 0) < iota((n, n), 1))
+        rank = jnp.sum(jnp.where(same, 1, 0), axis=0, keepdims=True)
+        slot = ids_ref[...] * 8 + rank
+        n_slots = out_ref.shape[0] * 8
+        placed = jnp.where(iota((n_slots, n), 0) == slot, 1.0, 0.0)
+        live = jnp.sum(placed, axis=1, keepdims=True)
+        routed = dot(placed.astype(BF16), embed)
+        out_ref[:, :, :D] = routed.reshape(n_slots // 8, 8, D).astype(BF16)
+        out_ref[:, :, D:] = jnp.broadcast_to(live, (n_slots, 128)).reshape(n_slots // 8, 8, 128).astype(BF16)
+
+
+def encode(pixels, encoder_ids, stem_weight, conv_weight, point_weight, proj_weight, n_tile, steps=4):
+    n = pixels.shape[0]
+    flat_pixels = pixels.reshape(n * 128, 384)
+    rows = n * 128 // steps
+    n_rows = rows // 16
+    stem_t = jnp.transpose(stem_weight, (0, 2, 1, 3))
+    whole = lambda shape: pl.BlockSpec(shape, lambda i: (0,) * len(shape))
+    return pl.pallas_call(
+        functools.partial(encode_kernel, steps),
+        grid=(steps,),
+        in_specs=[
+            pl.BlockSpec((rows, 384), lambda i: (i, 0)),
+            whole((1, n)),
+            whole(stem_t.shape),
+            whole(conv_weight.shape),
+            whole(point_weight.shape),
+            whole(proj_weight.shape),
+        ],
+        out_specs=whole((n_tile, 8, LINE)),
+        out_shape=jax.ShapeDtypeStruct((n_tile, 8, LINE), BF16),
+        scratch_shapes=[
+            pltpu.VMEM((64, 64), F32),
+            pltpu.VMEM((4, 256, 256), BF16),
+            pltpu.VMEM((3, 768, 256), BF16),
+            pltpu.VMEM((192, 256), BF16),
+            pltpu.VMEM((3, 6 * n_rows, 256), BF16),
+            pltpu.VMEM((3, 2 * n_rows, 768), BF16),
+            pltpu.VMEM((8 * n_rows, 128), BF16),
+            pltpu.VMEM((n, C3), BF16),
+        ],
+        name="encode_tiles",
+    )(flat_pixels, encoder_ids.reshape(1, n), stem_t, conv_weight, point_weight, proj_weight)
+
 ATTENTION_HEADS = 12
 HEAD_SIZE = 64
-
-
-def conv_stack(tiles, stem_weight, conv_weight, point_weight, proj_weight):
-    tile_count = tiles.shape[0]
-    tile_side = tiles.shape[1]
-    picture = tiles.reshape(tile_count, tile_side, tile_side, 3)
-    layout_spec = ("NHWC", "HWIO", "NHWC")
-    stem_out = lax.conv_general_dilated(
-        picture,
-        stem_weight,
-        (4, 4),
-        "VALID",
-        dimension_numbers=layout_spec,
-        preferred_element_type=jnp.float32,
-    )
-    stem_out = jax.nn.relu(stem_out).astype(jnp.bfloat16)
-    middle = lax.conv_general_dilated(
-        stem_out,
-        conv_weight,
-        (2, 2),
-        ((1, 1), (1, 1)),
-        dimension_numbers=layout_spec,
-        preferred_element_type=jnp.float32,
-    )
-    middle = jax.nn.relu(middle).astype(jnp.bfloat16)
-    point_out = jnp.einsum(
-        "nhwc,cd->nhwd", middle[:, ::2, ::2, :], point_weight, preferred_element_type=jnp.float32
-    )
-    pooled = jnp.mean(jax.nn.relu(point_out), axis=(1, 2)).astype(jnp.bfloat16)
-    return jnp.dot(pooled, proj_weight, preferred_element_type=jnp.float32).astype(jnp.bfloat16)
 
 
 def slide_layer(rows, live, qkv_weight, out_weight):
@@ -139,29 +279,10 @@
     pixels, encoder_ids, stem_weight, conv_weight, point_weight, proj_weight, qkv_weight, out_weight
 ):
     n_tile = lax.axis_size("tile")
-    tok_here = pixels.shape[0]
-    capacity = 2 * tok_here // n_tile
-    targets = encoder_ids[:, 0]
-    order = jnp.arange(tok_here, dtype=jnp.int32)
-    same = (targets[:, None] == targets[None, :]) & (order[None, :] < order[:, None])
-    ranks = jnp.sum(same.astype(jnp.int32), axis=1)
-    slots = targets * capacity + ranks
-    flags = (
-        jnp.zeros((n_tile * capacity,), jnp.bfloat16)
-        .at[slots]
-        .set(jnp.bfloat16(1.0))
-        .reshape(n_tile, capacity)
-    )
-    buffer = jnp.zeros((n_tile * capacity,) + pixels.shape[1:], jnp.bfloat16).at[slots].set(pixels)
-    buffer = buffer.reshape((n_tile, capacity) + pixels.shape[1:])
-    piece_pixels = lax.all_to_all(buffer, "tile", split_axis=0, concat_axis=0, tiled=True)
-    piece_flags = lax.all_to_all(flags, "tile", split_axis=0, concat_axis=0, tiled=True)
-    flat = piece_pixels.reshape((-1,) + piece_pixels.shape[2:])
-    embeds = conv_stack(flat, stem_weight, conv_weight, point_weight, proj_weight)
-    arrived = embeds.reshape(piece_pixels.shape[0], piece_pixels.shape[1], -1)
-    rows = arrived.reshape(n_tile * capacity, -1)
-    live = piece_flags.reshape(-1).astype(jnp.float32)
-    return slide_layer(rows, live, qkv_weight, out_weight)[None]
+    sent = encode(pixels, encoder_ids, stem_weight, conv_weight, point_weight, proj_weight, n_tile)
+    got = lax.all_to_all(sent, "tile", split_axis=0, concat_axis=0, tiled=True)
+    got = got.reshape(-1, LINE)
+    return slide_layer(got[:, :D], got[:, D].astype(F32), qkv_weight, out_weight)[None]
 
 
 def solution(mesh):

time: 383 us -> 123 us (0.32)
  waiting for transfers between devices: 156 us -> 0.01 us
  local copies, waits for them, and re-layouts: 101 us -> 28.5 us
  matrix products: 53.5 us -> 20.4 us
  Pallas kernels: 0 us -> 11.1 us
  starting transfers between devices: 15.2 us -> 8.46 us
    all_to_all x2 -> x1, waiting for transfers between devices: 156 us -> 0.01 us  [body(): got = lax.all_to_all(sent, 'tile', split_axis=0, concat_axis=0, tiled=True)]
    conv_general_dilated x1 -> x0, matrix products: 30.2 us -> none  [conv_stack(): lax.conv_general_dilated(stem_out, conv_weight, (2, 2), ((1, 1), (1, 1)),...]
    another operation x1 -> x0, local copies, waits for them, and re-layouts: 27.1 us -> none  [conv_stack(): picture = tiles.reshape(tile_count, tile_side, tile_side, 3)]
    scatter x2 -> x0, local copies, waits for them, and re-layouts: 21.1 us -> none  [the longest x1 20.1 us: body(): jnp.zeros((n_tile * capacity,) + pixels.shape[1:], jnp.bfloat16).at[slots]]
    all_to_all x3 -> x0, local copies, waits for them, and re-layouts: 17.5 us -> none  [the longest x1 16.7 us: body(): lax.all_to_all(buffer, 'tile', split_axis=0, concat_axis=0, tiled=True)]
    pallas_call x0 -> x1, Pallas kernels: none -> 11.1 us  [encode(): pl.pallas_call(functools.partial(encode_kernel, steps), grid=(steps,), in...]
    all_to_all x2 -> x1, starting transfers between devices: 15.2 us -> 8.46 us  [body(): got = lax.all_to_all(sent, 'tile', split_axis=0, concat_axis=0, tiled=True)]
    broadcast_in_dim x2 -> x0, local copies, waits for them, and re-layouts: 6.57 us -> none  [the longest x1 6.56 us: body(): jnp.zeros((n_tile * capacity,) + pixels.shape[1:], jnp.bfloat16).at[slots]]
  transfers between devices with their start and end apart: 2 -> 1, of which waited for: 1 -> 0; matrix products, arithmetic and copies ran while one was open for 10% -> 7% of each run, Pallas kernels for 0% -> 0%
where the time goes in v1:
time: 123 us; the launch traced here: 122 us
  blocking collectives  42.7 us (35%)
  local copies, waits for them, and re-layouts  28.5 us (23%)
  matrix products  20.4 us (17%)
  Pallas kernels  11.1 us (9%)
  other arithmetic  10.5 us (9%)
  starting transfers between devices  8.46 us (7%)
    all_gather x1, blocking collectives, slide_layer(): segment_keys = lax.all_gather(selected_keys, 'seq', axis=1, tiled=True)  15.9 us
    all_gather x1, blocking collectives, slide_layer(): piece_live = lax.all_gather(live_sel, 'seq', axis=1, tiled=True)  13.8 us
    all_gather x1, blocking collectives, slide_layer(): segment_values = lax.all_gather(values_sel, 'seq', axis=1, tiled=True)  13 us
    pallas_call x1, Pallas kernels, encode(): pl.pallas_call(functools.partial(encode_kernel, steps), grid=(steps,), in...  11.1 us
    all_to_all x1, starting transfers between devices, body(): got = lax.all_to_all(sent, 'tile', split_axis=0, concat_axis=0, tiled=True)  8.46 us
    mul x4, local copies, waits for them, and re-layouts, slide_layer(): context_sel[:, :, None, :] * choose  5.32 us
    slice x2, local copies, waits for them, and re-layouts, slide_layer(): keys_bf = packed[:, D:2 * D].astype(jnp.bfloat16)  2.56 us
  transfers between devices with their start and end apart: 1, of which 0 were waited for; matrix products, arithmetic and copies ran while one was open for 7% of the time, Pallas kernels for 0%

profile of v1, /device:TPU:1, one launch (start us, length us, event | category | flops | bytes accessed | tf_op | source)
XLA Modules:
  0.0 121.8 jit_solution(1696368325605851747)
XLA Ops:
  0.0 11.1 %encode_tiles.1 = bf16[16,8,896]{2,1,0:T(8,128)(2,1)} custom-call(bf16[8192,384]{1,0:T(8,128)(2,1)} %bitcast.63, s32[1,64]{1,0:T(1,128)} %bitcast.73, bf16[4,3,4,64]{3,2,1,0:T(4,128)(2,1)} %bitcast.72, bf16[3,3,64,128]{3,2,1,0:T(8,128)(2,1)} %conv_ref.1, bf16[128,256]{1,0:T(8,128)(2,1)} %point_ref.1, bf16[256,768]{1,0:T(8,128)(2,1)} %proj_ref.1), custom_call_target="tpu_custom_call" | custom-call | tf_op jit(solution)/shard_map/encode_tiles/pallas_call | solution.py:151
  11.1 8.5 %all-to-all-start = ((bf16[16,8,896]{2,1,0:T(8,128)(2,1)}), bf16[16,8,896]{2,1,0:T(8,128)(2,1)}, u32[]{:S(2)}, u32[]{:S(2)}) async-start(bf16[16,8,896]{2,1,0:T(8,128)(2,1)} %encode_tiles.1), calls=%async_computation | async-start | bytes 458752 | tf_op jit(solution)/shard_map/all_to_all | solution.py:283
  20.3 0.8 copy.42
  21.1 1.4 %copy.44 = pred[8,12,1]{0,2,1:T(4,128)(4,1)} copy(pred[8,12,1]{1,0,2:T(8,128)(4,1)} %get-tuple-element.14) | data formatting | bytes 192 | tf_op jit(solution)/shard_map/eq | solution.py:210
  22.4 0.6 mul.103
  23.1 1.6 %mul.104 = f32[12,128]{1,0:T(8,128)} reshape(f32[12,16,8]{2,1,0:T(8,128)} %mul.103) | data formatting | bytes 12288 | tf_op jit(solution)/shard_map/mul | solution.py:268
  24.7 0.7 fusion.28
  25.4 0.6 mul.116
  26.1 1.6 %mul.117 = f32[12,128]{1,0:T(8,128)} reshape(f32[12,16,8]{2,1,0:T(8,128)} %mul.116) | data formatting | bytes 12288 | tf_op jit(solution)/shard_map/mul | solution.py:268
  27.6 1.0 fusion.9
  28.7 1.4 %slice_reduce_fusion = (bf16[128]{0:T(256)(128)(2,1)S(1)}, bf16[128,1]{1,0:T(8,128)(2,1)}) fusion(bf16[128,896]{1,0:T(8,128)(2,1)} %bitcast.3), kind=kLoop, calls=%fused_computation.57 | loop fusion | bytes 768
  30.1 1.6 %convolution_convert_fusion = bf16[128,2304]{1,0:T(8,128)(2,1)S(1)} fusion(bf16[768,2304]{1,0:T(8,128)(2,1)S(1)} %copy-done, f32[128]{0:T(128)S(1)} %add_rsqrt_fusion, bf16[128,896]{1,0:T(8,128)(2,1)} %bitcast.3), kind=kOutput, calls=%fused_computation | convolution fusion | flops 453574656 | bytes 4325888 | tf_op jit(solution)/shard_map/dot_general | solution.py:188
  31.7 0.8 fusion.37
  32.5 2.1 %reshape_reshape.9 = bf16[16,8,12,64]{3,2,1,0:T(8,128)(2,1)} reshape(bf16[128,768]{1,0:T(8,128)(2,1)} %get-tuple-element.11) | data formatting | bytes 393216 | tf_op jit(solution)/shard_map/reshape;reshape | solution.py:215
  34.6 1.7 %copy.33 = bf16[128,768]{0,1:T(8,128)(2,1)} copy(bf16[128,768]{1,0:T(8,128)(2,1)} %get-tuple-element.11) | data formatting | bytes 393216 | tf_op jit(solution)/shard_map/slice | solution.py:190
  36.3 2.1 %reshape_reshape.10 = bf16[16,8,12,64]{3,2,1,0:T(8,128)(2,1)} reshape(bf16[128,768]{1,0:T(8,128)(2,1)} %get-tuple-element.9) | data formatting | bytes 393216 | tf_op jit(solution)/shard_map/reshape;reshape | solution.py:220
  38.4 1.7 %copy.34 = bf16[128,768]{0,1:T(8,128)(2,1)} copy(bf16[128,768]{1,0:T(8,128)(2,1)} %get-tuple-element.9) | data formatting | bytes 393216 | tf_op jit(solution)/shard_map/slice | solution.py:195
  40.1 1.7 %copy.35 = bf16[128,768]{0,1:T(8,128)(2,1)} copy(bf16[128,768]{1,0:T(8,128)(2,1)} %get-tuple-element.10) | data formatting | bytes 393216 | tf_op jit(solution)/shard_map/slice | solution.py:196
  41.9 2.1 %reshape_reshape.11 = bf16[16,8,12,64]{3,2,1,0:T(8,128)(2,1)} reshape(bf16[128,768]{1,0:T(8,128)(2,1)} %get-tuple-element.10) | data formatting | bytes 393216 | tf_op jit(solution)/shard_map/reshape;reshape | solution.py:225
  43.9 0.8 copy.53
  45.9 1.3 %fusion.13 = f32[12,1,16,64]{3,1,2,0:T(1,128)S(1)} fusion(pred[8,12,1,1]{0,2,3,1:T(4,128)(4,1)S(1)} %copy.42, bf16[16,8,12,64]{3,2,1,0:T(8,128)(2,1)} %reshape_reshape.10), kind=kOutput, calls=%fused_computation.22 | convolution fusion | flops 196608 | bytes 245856 | tf_op jit(solution)/shard_map/bnpo,np->pbo/dot_general | solution.py:218
  47.2 15.9 %all_gather.10 = bf16[12,128,64]{2,1,0:T(8,128)(2,1)} all-gather(bf16[12,16,64]{2,1,0:T(8,128)(2,1)S(1)} %convert_element_type.79), channel_id=1, replica_groups=mesh['tile'=16,'seq'=8] {'seq'}, dimensions={1}, use_global_device_ids=true | all-gather | bytes 221184 | tf_op jit(solution)/shard_map/all_gather | solution.py:246
  63.1 1.9 %fusion.15 = f32[12,1,16,64]{3,1,2,0:T(1,128)} fusion(pred[8,12,1,1]{0,2,3,1:T(4,128)(4,1)S(1)} %copy.42, bf16[16,8,12,64]{3,2,1,0:T(8,128)(2,1)} %reshape_reshape.9), kind=kOutput, calls=%fused_computation.24 | convolution fusion | flops 196608 | bytes 245856 | tf_op jit(solution)/shard_map/bnpo,np->pbo/dot_general | solution.py:213
  65.2 0.9 convolution_convert_fusion.1
  66.1 13.8 %all_gather.9 = bf16[12,128]{0,1:T(8,128)(2,1)} all-gather(bf16[12,16]{0,1:T(8,128)(2,1)S(1)} %copy.38), channel_id=1, replica_groups=mesh['tile'=16,'seq'=8] {'seq'}, dimensions={1}, use_global_device_ids=true | all-gather | bytes 3456 | tf_op jit(solution)/shard_map/all_gather | solution.py:248
  80.0 0.8 copy.39
  80.8 0.6 fusion.36
  81.4 1.4 %fusion.34 = (f32[128,128]{0,1:T(8,128)}, pred[128,128]{0,1:T(8,128)(4,1)S(1)}) fusion(pred[128]{0:T(512)(128)(4,1)} %compare_bitcast_fusion), kind=kLoop, calls=%fused_computation.54 | loop fusion | flops 49152 | bytes 82048 | tf_op jit(solution)/shard_map/convert_element_type | solution.py:206
  82.8 2.2 %fusion.38 = (f32[12,128]{1,0:T(8,128)S(1)}, f32[12,128,128]{1,2,0:T(8,128)}) fusion(bf16[128,12,64]{0,2,1:T(8,128)(2,1)} %bitcast.64, bf16[128,12,64]{0,2,1:T(8,128)(2,1)} %bitcast.65, pred[128,128]{0,1:T(8,128)(4,1)S(1)} %get-tuple-element.17), kind=kOutput, calls=%fused_computation.60 | convolution fusion | flops 25754112 | bytes 1202176 | tf_op jit(solution)/shard_map/phd,qhd->hpq/dot_general | solution.py:200
  85.0 0.7 reshape.175
  85.8 1.3 %fusion.7 = f32[12,128]{1,0:T(8,128)S(1)} fusion(f32[12,128,128]{1,2,0:T(8,128)} %get-tuple-element.19, f32[128,128]{0,1:T(8,128)} %get-tuple-element.16, f32[12,128]{1,0:T(8,128)S(1)} %get-tuple-element.18), kind=kLoop, calls=%fused_computation.14 | loop fusion | flops 588288 | bytes 864256 | tf_op jit(solution)/shard_map/reduce_sum | solution.py:207
  87.0 0.7 reshape.177
  87.8 1.5 %fusion.40 = f32[12,1,16]{2,1,0:T(1,128)} fusion(bf16[12,16,8]{2,1,0:T(8,128)(2,1)} %reshape.175, pred[8,12,1]{0,2,1:T(4,128)(4,1)} %copy.44), kind=kOutput, calls=%fused_computation.62 | convolution fusion | flops 3072 | bytes 3936 | tf_op jit(solution)/shard_map/hmr,rh->hm/dot_general | solution.py:231
  89.3 1.5 %fusion.41 = f32[12,1,16]{2,1,0:T(1,128)} fusion(bf16[12,16,8]{2,1,0:T(8,128)(2,1)} %reshape.177, pred[8,12,1]{0,2,1:T(4,128)(4,1)} %copy.44), kind=kOutput, calls=%fused_computation.63 | convolution fusion | flops 3072 | bytes 3936 | tf_op jit(solution)/shard_map/hmr,rh->hm/dot_general | solution.py:236
  90.8 2.2 %fusion.8 = f32[12,128,64]{1,2,0:T(8,128)} fusion(bf16[128,12,64]{0,2,1:T(8,128)(2,1)} %bitcast.66, f32[12,128,128]{1,2,0:T(8,128)} %get-tuple-element.19, f32[128,128]{0,1:T(8,128)} %get-tuple-element.16, f32[12,128]{1,0:T(8,128)S(1)} %get-tuple-element.18), kind=kOutput, calls=%fused_computation.15 | convolution fusion | flops 25559040 | bytes 1447936 | tf_op jit(solution)/shard_map/hpq,qhd->hpd/dot_general | solution.py:208
  93.0 1.9 %copy.37 = bf16[12,128,64]{2,1,0:T(8,128)(2,1)} copy(f32[12,128,64]{1,2,0:T(8,128)} %fusion.8) | data formatting | bytes 589824 | tf_op jit(solution)/shard_map/hpq,qhd->hpd/dot_general | solution.py:208
  95.0 1.2 %fusion.5 = f32[12,1,16,64]{3,1,2,0:T(1,128)S(1)} fusion(pred[8,12,1,1]{0,2,3,1:T(4,128)(4,1)} %copy-done.2, bf16[12,128,64]{2,1,0:T(8,128)(2,1)} %copy.37), kind=kOutput, calls=%fused_computation.11 | convolution fusion | flops 196608 | bytes 245856 | tf_op jit(solution)/shard_map/bstc,tb->bsc/dot_general | solution.py:241
  96.2 1.3 %fusion.11 = f32[12,1,16,64]{3,1,2,0:T(1,128)S(1)} fusion(pred[8,12,1,1]{0,2,3,1:T(4,128)(4,1)} %copy-done.2, bf16[16,8,12,64]{3,2,1,0:T(8,128)(2,1)} %reshape_reshape.11), kind=kOutput, calls=%fused_computation.20 | convolution fusion | flops 196608 | bytes 245856 | tf_op jit(solution)/shard_map/bnpo,np->pbo/dot_general | solution.py:223
  97.5 13.0 %all_gather.11 = bf16[12,128,64]{2,1,0:T(8,128)(2,1)S(1)} all-gather(bf16[12,16,64]{2,1,0:T(8,128)(2,1)S(1)} %convert_element_type.81), channel_id=1, replica_groups=mesh['tile'=16,'seq'=8] {'seq'}, dimensions={1}, use_global_device_ids=true | all-gather | bytes 221184 | tf_op jit(solution)/shard_map/all_gather | solution.py:247
  110.5 1.4 %fusion.39 = (f32[12,16]{1,0:T(8,128)S(1)}, f32[12,16,128]{2,1,0:T(8,128)S(1)}) fusion(f32[12,16,64]{2,1,0:T(8,128)} %bitcast.68, bf16[12,128,64]{2,1,0:T(8,128)(2,1)} %all_gather.10, pred[12,128]{1,0:T(8,128)(4,1)} %get-tuple-element.8), kind=kOutput, calls=%fused_computation.61 | convolution fusion | flops 3219264 | bytes 346368 | tf_op jit(solution)/shard_map/psi,pei->pse/dot_general | solution.py:251
  111.9 0.7 bitcast_maximum_fusion
  112.6 0.9 fusion.22
  113.5 0.7 fusion.26
  114.2 1.0 fusion.4
  115.2 1.0 broadcast_bitcast_fusion
  116.2 2.1 %copy.40 = f32[12,128,64]{1,2,0:T(8,128)} copy(f32[12,128,64]{2,1,0:T(8,128)} %broadcast_bitcast_fusion) | data formatting | bytes 786432 | tf_op jit(solution)/shard_map/mul | solution.py:268
  118.3 1.2 add_convert_fusion
  119.5 2.3 %fusion.2 = bf16[1,128,768]{2,1,0:T(8,128)(2,1)} fusion(bf16[128,768]{0,1:T(8,128)(2,1)S(1)} %bitcast.67, bf16[768,768]{1,0:T(8,128)(2,1)} %param.15, f32[128]{0:T(128)} %convert_bitcast_fusion), kind=kOutput, calls=%fused_computation.5 | convolution fusion | flops 151191552 | bytes 1573376 | tf_op jit(solution)/shard_map/dot_general | solution.py:274
  (19 shorter events, 2.1 us)
Async XLA Ops:
  0.0 30.1 %copy-start = (bf16[768,2304]{1,0:T(8,128)(2,1)S(1)}, bf16[768,2304]{1,0:T(8,128)(2,1)}, u32[]{:S(2)}) copy-start(bf16[768,2304]{1,0:T(8,128)(2,1)} %param.14) | copy-start | bytes 10616836
  11.1 16.5 %all-to-all-start = ((bf16[16,8,896]{2,1,0:T(8,128)(2,1)}), bf16[16,8,896]{2,1,0:T(8,128)(2,1)}, u32[]{:S(2)}, u32[]{:S(2)}) async-start(bf16[16,8,896]{2,1,0:T(8,128)(2,1)} %encode_tiles.1), calls=%async_computation | async-start | bytes 458752 | tf_op jit(solution)/shard_map/all_to_all | solution.py:283
  19.6 0.7 copy-start.3
  21.1 42.1 %copy-start.2 = (pred[8,12,1,1]{0,2,3,1:T(4,128)(4,1)}, pred[8,12,1,1]{0,2,3,1:T(4,128)(4,1)S(1)}, u32[]{:S(2)}) copy-start(pred[8,12,1,1]{0,2,3,1:T(4,128)(4,1)S(1)} %copy.42) | copy-start | bytes 292
  93.0 25.3 %copy-start.1 = (f32[12,128]{1,0:T(8,128)S(1)}, f32[12,128]{1,0:T(8,128)}, u32[]{:S(2)}) copy-start(f32[12,128]{1,0:T(8,128)} %mul.104) | copy-start | bytes 18436

commit v2 on v1

--- a/solution.py
+++ b/solution.py
@@ -10,7 +10,9 @@
 C1, C2, C3 = 64, 128, 256
 GROUP = 16
 LINE = D + 128
+HEAD_SIZE = 64
 F32, BF16 = jnp.float32, jnp.bfloat16
+MESH = pl.DeviceIdType.MESH
 
 BLOCKS = (
     ((0, 0, 1), (1, 0, 2), (3, 1, 0), (4, 1, 1)),
@@ -174,105 +176,158 @@
         name="encode_tiles",
     )(flat_pixels, encoder_ids.reshape(1, n), stem_t, conv_weight, point_weight, proj_weight)
 
-ATTENTION_HEADS = 12
-HEAD_SIZE = 64
-
-
-def slide_layer(rows, live, qkv_weight, out_weight):
-    sequence_count = lax.axis_size("seq")
-    seg_len = rows.shape[0]
-    dilation_groups = seg_len // sequence_count
-    wide = rows.astype(jnp.float32)
-    power = jnp.mean(wide * wide, axis=-1, keepdims=True)
-    normed = (wide * lax.rsqrt(power + 1e-06)).astype(jnp.bfloat16)
-    packed = jnp.dot(normed, qkv_weight, preferred_element_type=jnp.float32)
-    query_rows = (
-        packed[:, :D]
-        .astype(jnp.bfloat16)
-        .astype(jnp.float32)
-        .reshape(seg_len, ATTENTION_HEADS, HEAD_SIZE)
-    )
-    keys_bf = packed[:, D : 2 * D].astype(jnp.bfloat16)
-    values_bf = packed[:, 2 * D :].astype(jnp.bfloat16)
-    key_rows = keys_bf.astype(jnp.float32).reshape(seg_len, ATTENTION_HEADS, HEAD_SIZE)
-    value_rows = values_bf.astype(jnp.float32).reshape(seg_len, ATTENTION_HEADS, HEAD_SIZE)
-    score_scale = 1.0 / jnp.sqrt(jnp.float32(HEAD_SIZE))
-    scores = jnp.einsum("phd,qhd->hpq", query_rows, key_rows) * score_scale
-    places = jnp.arange(seg_len)
-    alive = live > 0.5
-    local = alive[None, :] | (places[:, None] == places[None, :])
-    masked = jnp.where(local[None], scores, jnp.float32(-1e30))
-    top_local = jnp.max(masked, axis=-1)
-    weights = jnp.exp(masked - top_local[:, :, None]) * local[None].astype(jnp.float32)
-    den_local = jnp.sum(weights, axis=-1)
-    local_accumulator = jnp.einsum("hpq,qhd->hpd", weights, value_rows)
-    offsets = jnp.arange(ATTENTION_HEADS) % sequence_count
-    dilation_selector = (jnp.arange(sequence_count)[:, None] == offsets[None, :]).astype(
-        jnp.float32
-    )
-    selected_query = jnp.einsum(
-        "bnpo,np->pbo",
-        query_rows.reshape(dilation_groups, sequence_count, ATTENTION_HEADS, HEAD_SIZE),
-        dilation_selector,
-    )
-    selected_keys = jnp.einsum(
-        "bnpo,np->pbo",
-        key_rows.reshape(dilation_groups, sequence_count, ATTENTION_HEADS, HEAD_SIZE),
-        dilation_selector,
-    ).astype(jnp.bfloat16)
-    values_sel = jnp.einsum(
-        "bnpo,np->pbo",
-        value_rows.reshape(dilation_groups, sequence_count, ATTENTION_HEADS, HEAD_SIZE),
-        dilation_selector,
-    ).astype(jnp.bfloat16)
-    live_sel = jnp.einsum(
-        "mr,rh->hm", live.reshape(dilation_groups, sequence_count), dilation_selector
-    ).astype(jnp.bfloat16)
-    start_top = jnp.einsum(
-        "hmr,rh->hm",
-        top_local.reshape(ATTENTION_HEADS, dilation_groups, sequence_count),
-        dilation_selector,
-    )
-    start_den = jnp.einsum(
-        "hmr,rh->hm",
-        den_local.reshape(ATTENTION_HEADS, dilation_groups, sequence_count),
-        dilation_selector,
-    )
-    initial_accumulator = jnp.einsum(
-        "bstc,tb->bsc",
-        local_accumulator.reshape(ATTENTION_HEADS, dilation_groups, sequence_count, HEAD_SIZE),
-        dilation_selector,
-    )
-    segment_keys = lax.all_gather(selected_keys, "seq", axis=1, tiled=True)
-    segment_values = lax.all_gather(values_sel, "seq", axis=1, tiled=True)
-    piece_live = lax.all_gather(live_sel, "seq", axis=1, tiled=True)
-    usable = piece_live.astype(jnp.float32) > 0.5
-    partial_scores = (
-        jnp.einsum("psi,pei->pse", selected_query, segment_keys.astype(jnp.float32)) * score_scale
-    )
-    part_masked = jnp.where(usable[:, None, :], partial_scores, jnp.float32(-1e30))
-    new_top = jnp.maximum(start_top, jnp.max(part_masked, axis=-1))
-    rescale = jnp.exp(start_top - new_top)
-    partial_weights = jnp.exp(part_masked - new_top[:, :, None]) * usable[:, None, :].astype(
-        jnp.float32
-    )
-    new_den = start_den * rescale + jnp.sum(partial_weights, axis=-1)
-    new_acc = initial_accumulator * rescale[:, :, None] + jnp.einsum(
-        "zfj,zjg->zfg", partial_weights, segment_values.astype(jnp.float32)
-    )
-    context_sel = new_acc / new_den[:, :, None]
-    context_local = (local_accumulator / den_local[:, :, None]).reshape(
-        ATTENTION_HEADS, dilation_groups, sequence_count, HEAD_SIZE
-    )
-    choose = jnp.transpose(dilation_selector, (1, 0))[:, None, :, None]
-    context = context_local * (1.0 - choose) + context_sel[:, :, None, :] * choose
-    context = (
-        jnp.transpose(context.reshape(ATTENTION_HEADS, seg_len, HEAD_SIZE), (1, 0, 2))
-        .reshape(seg_len, D)
-        .astype(jnp.bfloat16)
-    )
-    result = jnp.dot(context, out_weight, preferred_element_type=jnp.float32) * live[:, None]
-    return result.astype(jnp.bfloat16)
+
+def spread_rows(n, minor):
+    row, col = iota((n, n), 0), iota((n, n), 1)
+    shift = minor.bit_length() - 1
+    return jnp.where(col == (row & (minor - 1)) * (n // minor) + (row >> shift), 1.0, 0.0).astype(BF16)
+
+
+def dot_t(a, b):
+    return lax.dot_general(a, b, (((1,), (1,)), ((), ())), preferred_element_type=F32)
+
+
+def layer_kernel(n_tile, n_seq, sent, qkv_hbm, out_hbm, o_ref, got, qkv_w, out_w, kv_send, kv_all, context,
+                 weight_sem, own_sem, send_sem, recv_sem, kv_send_sem, kv_recv_sem):
+    t, s = lax.axis_index("tile"), lax.axis_index("seq")
+    load_qkv = pltpu.make_async_copy(qkv_hbm, qkv_w, weight_sem.at[0])
+    load_out = pltpu.make_async_copy(out_hbm, out_w, weight_sem.at[1])
+    load_qkv.start()
+    load_out.start()
+    barrier = pltpu.get_barrier_semaphore()
+    for k in range(1, n_tile):
+        pl.semaphore_signal(barrier, inc=1, device_id={"tile": lax.rem(t + k, n_tile)}, device_id_type=MESH)
+    for k in range(1, n_seq):
+        pl.semaphore_signal(barrier, inc=1, device_id={"seq": lax.rem(s + k, n_seq)}, device_id_type=MESH)
+    keep = pltpu.make_async_copy(sent.at[t], got.at[t], own_sem)
+    keep.start()
+    pl.semaphore_wait(barrier, n_tile + n_seq - 2)
+    moves = []
+    for k in range(1, n_tile):
+        peer = lax.rem(t + k, n_tile)
+        moves.append(pltpu.make_async_remote_copy(
+            src_ref=sent.at[peer], dst_ref=got.at[t], send_sem=send_sem.at[k - 1], recv_sem=recv_sem.at[k - 1],
+            device_id={"tile": peer}, device_id_type=MESH))
+        moves[-1].start()
+    n = n_tile * 8
+    low = iota((n, 128), 1) < HEAD_SIZE
+    keep.wait()
+    for move in moves:
+        move.wait()
+
+    natural = got[...].astype(F32).reshape(n, LINE)
+    rows = dot(spread_rows(n, n_tile), natural.astype(BF16))
+    live = rows[:, D:]
+    rows = rows[:, :D]
+    power = jnp.mean(rows * rows, axis=-1, keepdims=True)
+    normed = (rows * lax.rsqrt(power + 1e-06)).astype(BF16)
+    load_qkv.wait()
+    pairs = D // 128
+    kv = dot(normed, qkv_w[:, D:]).astype(BF16)
+    low16 = low[:n_tile]
+
+    def offsets(m):
+        a = (2 * m) % n_seq
+        b = (2 * m + 1) % n_seq
+        return slice(a * n_tile, (a + 1) * n_tile), slice(b * n_tile, (b + 1) * n_tile)
+
+    for m in range(2 * pairs):
+        chunk = kv[:, m * 128:(m + 1) * 128]
+        first, second = offsets(m % pairs)
+        kv_send[m] = jnp.where(low16, chunk[first], chunk[second])
+    flags = jnp.zeros((n_tile, 128), F32)
+    for r in range(n_seq):
+        flags = jnp.where(iota((n_tile, 128), 1) == r, live[r * n_tile:(r + 1) * n_tile], flags)
+    kv_send[2 * pairs] = flags.astype(BF16)
+    kv_moves = []
+    for k in range(1, n_seq):
+        peer = lax.rem(s + k, n_seq)
+        kv_moves.append(pltpu.make_async_remote_copy(
+            src_ref=kv_send, dst_ref=kv_all.at[s], send_sem=kv_send_sem.at[k - 1], recv_sem=kv_recv_sem.at[k - 1],
+            device_id={"seq": peer}, device_id_type=MESH))
+        kv_moves[-1].start()
+    kv_all[s] = kv_send[...]
+
+    query = (dot(normed, qkv_w[:, :D]).astype(BF16) * 0.125).astype(BF16)
+    live_across = jnp.transpose(live)
+    own = iota((n, n), 0) == iota((n, n), 1)
+    bias = jnp.where((live_across > 0.5) | own, 0.0, -1e30)
+    bias = jnp.concatenate([bias, bias], axis=0)
+    none = jnp.zeros((n, 128), BF16)
+    kept = []
+    for m in range(pairs):
+        lanes = slice(m * 128, (m + 1) * 128)
+        q = query[:, lanes]
+        q = jnp.concatenate([jnp.where(low, q, none), jnp.where(low, none, q)], axis=0)
+        score = dot_t(q, kv[:, lanes]) + bias
+        top = jnp.max(score, axis=-1, keepdims=True)
+        weight = jnp.exp(score - top)
+        total = jnp.sum(weight, axis=-1, keepdims=True)
+        summed = dot(weight.astype(BF16), kv[:, D + m * 128:D + (m + 1) * 128])
+        result = summed / total
+        context[:, lanes] = jnp.where(low, result[:n], result[n:]).astype(BF16)
+        first, second = offsets(m)
+        second = slice(n + second.start, n + second.stop)
+        kept.append([jnp.concatenate([x[first], x[second]], axis=0) for x in (q, top, total, summed)])
+
+    for move in kv_moves:
+        move.wait()
+    there = kv_all[:, 2 * pairs].reshape(n, 128)
+    pick = jnp.where(iota((n_tile, 128), 0) == iota((n_tile, 128), 1), 1.0, 0.0).astype(BF16)
+    far_bias = jnp.where(dot_t(pick, there) > 0.5, 0.0, -1e30)
+    for m in range(pairs):
+        lanes = slice(m * 128, (m + 1) * 128)
+        first, second = offsets(m)
+        q, top, total, summed = kept[m]
+        a, b = first.start // n_tile, second.start // n_tile
+        far = jnp.concatenate([jnp.broadcast_to(far_bias[a:a + 1], (n_tile, 128)),
+                               jnp.broadcast_to(far_bias[b:b + 1], (n_tile, 128))], axis=0)
+        score = dot_t(q, kv_all[:, m].reshape(n, 128)) + far
+        new_top = jnp.maximum(top, jnp.max(score, axis=-1, keepdims=True))
+        weight = jnp.exp(score - new_top)
+        scale = jnp.exp(top - new_top)
+        total = total * scale + jnp.sum(weight, axis=-1, keepdims=True)
+        summed = summed * scale + dot(weight.astype(BF16), kv_all[:, pairs + m].reshape(n, 128))
+        result = (summed / total).astype(BF16)
+        context[first, lanes] = jnp.where(low16, result[:n_tile], context[first, lanes])
+        context[second, lanes] = jnp.where(low16, context[second, lanes], result[n_tile:])
+
+    back = dot(spread_rows(n, n_seq), context[...]).astype(BF16)
+    load_out.wait()
+    final = dot(back, out_w[...])
+    alive = natural[:, D:] > 0.5
+    for m in range(pairs):
+        lanes = slice(m * 128, (m + 1) * 128)
+        o_ref[:, lanes] = jnp.where(alive, final[:, lanes], 0.0).astype(BF16)
+
+
+def slide_layer(sent, qkv_weight, out_weight):
+    n_tile, n_seq = lax.axis_size("tile"), lax.axis_size("seq")
+    n = n_tile * 8
+    anywhere = pl.BlockSpec(memory_space=pl.ANY)
+    blocks = 2 * D // 128 + 1
+    return pl.pallas_call(
+        functools.partial(layer_kernel, n_tile, n_seq),
+        in_specs=[anywhere] * 3,
+        out_specs=pl.BlockSpec(memory_space=pltpu.VMEM),
+        out_shape=jax.ShapeDtypeStruct((n, D), BF16),
+        scratch_shapes=[
+            pltpu.VMEM((n_tile, 8, LINE), BF16),
+            pltpu.VMEM(qkv_weight.shape, BF16),
+            pltpu.VMEM(out_weight.shape, BF16),
+            pltpu.VMEM((blocks, n_tile, 128), BF16),
+            pltpu.VMEM((n_seq, blocks, n_tile, 128), BF16),
+            pltpu.VMEM((n, D), BF16),
+            pltpu.SemaphoreType.DMA((2,)),
+            pltpu.SemaphoreType.DMA,
+            pltpu.SemaphoreType.DMA((n_tile - 1,)),
+            pltpu.SemaphoreType.DMA((n_tile - 1,)),
+            pltpu.SemaphoreType.DMA((n_seq - 1,)),
+            pltpu.SemaphoreType.DMA((n_seq - 1,)),
+        ],
+        compiler_params=pltpu.CompilerParams(collective_id=0, has_side_effects=True),
+        name="slide_layer",
+    )(sent, qkv_weight, out_weight)
 
 
 def body(
@@ -280,9 +335,7 @@
 ):
     n_tile = lax.axis_size("tile")
     sent = encode(pixels, encoder_ids, stem_weight, conv_weight, point_weight, proj_weight, n_tile)
-    got = lax.all_to_all(sent, "tile", split_axis=0, concat_axis=0, tiled=True)
-    got = got.reshape(-1, LINE)
-    return slide_layer(got[:, :D], got[:, D].astype(F32), qkv_weight, out_weight)[None]
+    return slide_layer(sent, qkv_weight, out_weight)[None]
 
 
 def solution(mesh):

time: 123 us -> 36.5 us (0.30)
  blocking collectives: 42.7 us -> 0 us
  local copies, waits for them, and re-layouts: 28.5 us -> 1.62 us
  Pallas kernels: 11.1 us -> 34.7 us
  matrix products: 20.4 us -> 0 us
  other arithmetic: 10.5 us -> 0 us
  starting transfers between devices: 8.46 us -> 0 us
    all_gather x3 -> x0, blocking collectives: 42.7 us -> none  [the longest x1 15.9 us: slide_layer(): segment_keys = lax.all_gather(selected_keys, 'seq', axis=1, tiled=True)]
    pallas_call x0 -> x1, Pallas kernels: none -> 23.8 us  [slide_layer(): pl.pallas_call(functools.partial(layer_kernel, n_tile, n_seq), in_specs=[...]
    dot_general x13 -> x0, matrix products: 20.4 us -> none  [the longest x1 2.3 us: slide_layer(): jnp.dot(context, out_weight, preferred_element_type=jnp.float32)]
    all_to_all x1 -> x0, starting transfers between devices: 8.46 us -> none  [body(): got = lax.all_to_all(sent, 'tile', split_axis=0, concat_axis=0, tiled=True)]
    mul x6 -> x0, local copies, waits for them, and re-layouts: 7.55 us -> none  [the longest x4 5.32 us: slide_layer(): context_sel[:, :, None, :] * choose]
    another operation x3 -> x0, local copies, waits for them, and re-layouts: 6.21 us -> none  [the longest x1 2.09 us: slide_layer(): key_rows.reshape(dilation_groups, sequence_count, ATTENTION_HEADS, HEAD_S...]
    slice x4 -> x0, local copies, waits for them, and re-layouts: 6.04 us -> none  [the longest x2 2.56 us: slide_layer(): keys_bf = packed[:, D:2 * D].astype(jnp.bfloat16)]
    convert_element_type x6 -> x0, other arithmetic: 3.99 us -> none  [the longest x1 1.39 us: slide_layer(): local[None].astype(jnp.float32)]
  transfers between devices with their start and end apart: 1 -> 0, of which waited for: 0 -> 0; matrix products, arithmetic and copies ran while one was open for 7% -> 0% of each run, Pallas kernels for 0% -> 0%
where the time goes in v2:
time: 36.5 us; the launch traced here: 36.4 us
  Pallas kernels  34.7 us (95%)
  local copies, waits for them, and re-layouts  1.62 us (4%)
    pallas_call x1, Pallas kernels, slide_layer(): pl.pallas_call(functools.partial(layer_kernel, n_tile, n_seq), in_specs=[...  23.8 us
    pallas_call x1, Pallas kernels, encode(): pl.pallas_call(functools.partial(encode_kernel, steps), grid=(steps,), in...  10.9 us
    unnamed x1, local copies, waits for them, and re-layouts  1.62 us

profile of v2, /device:TPU:1, one launch (start us, length us, event | category | flops | bytes accessed | tf_op | source)
XLA Modules:
  0.0 36.4 jit_solution(16192382996242020085)
XLA Ops:
  0.0 10.9 %encode_tiles.1.sent = bf16[16,8,896]{2,1,0:T(8,128)(2,1)} custom-call(bf16[8192,384]{1,0:T(8,128)(2,1)} %bitcast.4, s32[1,64]{1,0:T(1,128)} %bitcast.7, bf16[4,3,4,64]{3,2,1,0:T(4,128)(2,1)} %bitcast.6, bf16[3,3,64,128]{3,2,1,0:T(8,128)(2,1)} %conv_ref.1, bf16[128,256]{1,0:T(8,128)(2,1)} %point_ref.1, bf16[256,768]{1,0:T(8,128)(2,1)} %proj_ref.1), custom_call_target="tpu_custom_call" | custom-call | tf_op jit(solution)/shard_map/encode_tiles/pallas_call | solution.py:153
  10.9 23.8 %slide_layer.1 = bf16[128,768]{1,0:T(8,128)(2,1)} custom-call(bf16[16,8,896]{2,1,0:T(8,128)(2,1)} %encode_tiles.1.sent, bf16[768,2304]{1,0:T(8,128)(2,1)} %qkv_hbm.1, bf16[768,768]{1,0:T(8,128)(2,1)} %out_hbm.1), custom_call_target="tpu_custom_call" | custom-call | tf_op jit(solution)/shard_map/slide_layer/pallas_call | solution.py:309
  34.8 1.6 %copy.10 = bf16[1,128,768]{2,1,0:T(8,128)(2,1)} copy(bf16[1,128,768]{2,1,0:T(8,128)(2,1)} %bitcast.5) | data formatting | bytes 393216

commit v3 on v2

--- a/solution.py
+++ b/solution.py
@@ -51,36 +51,32 @@
     return jnp.where((lane >= first) & (lane < first + 12), spread, 0.0).astype(BF16)
 
 
-def encode_kernel(steps, pix_ref, ids_ref, stem_ref, conv_ref, point_ref, proj_ref, out_ref,
-                  flat, stem_w, conv_w, picked, packed, hidden, middle, pooled):
-    step = pl.program_id(0)
-    n_tiles = pix_ref.shape[0] // 128
+def prepare(stem_ref, conv_ref, flat, stem_w, conv_w, picked):
+    flat[...] = jnp.zeros_like(flat)
+    for a in range(4):
+        for c in range(3):
+            flat[a * 16 + c * 4:a * 16 + c * 4 + 4, :] = stem_ref[a, c].astype(F32)
+    for base, uses in ((0, ((0, 0), (1, 1))), (64, ((2, 1),)), (128, ((3, 2),))):
+        spread = stem_spread(stem_ref, flat, base)
+        for slot, block in uses:
+            stem_w[slot] = stem_block(spread, base, BLOCKS[block])
+    conv_w[...] = jnp.zeros_like(conv_w)
+    for n, block in enumerate(BLOCKS):
+        for d in range(3):
+            for q, (_, side, tap) in enumerate(block):
+                row = d * 256 + q * 64
+                conv_w[n, row:row + 64, side * 128:side * 128 + 128] = conv_ref[d, tap]
+    row, col = iota((192, 256), 0), iota((192, 256), 1)
+    tap_row, g = row >> 4, row & 15
+    a, d = tap_row & 3, tap_row >> 2
+    row_of = 16 * g + 4 * (d - 1) + a
+    good = (row_of == col) & ((d > 0) | ((g & 7) > 0))
+    picked[...] = jnp.where(good, 1.0, 0.0).astype(BF16)
+
+
+def encode_step(step, n_tiles, pix_ref, point_ref, stem_w, conv_w, picked, packed, hidden, middle, pooled):
     n_blocks = n_tiles // 2
     n_rows = n_tiles * 8
-
-    @pl.when(step == 0)
-    def _():
-        flat[...] = jnp.zeros_like(flat)
-        for a in range(4):
-            for c in range(3):
-                flat[a * 16 + c * 4:a * 16 + c * 4 + 4, :] = stem_ref[a, c].astype(F32)
-        for base, uses in ((0, ((0, 0), (1, 1))), (64, ((2, 1),)), (128, ((3, 2),))):
-            spread = stem_spread(stem_ref, flat, base)
-            for slot, block in uses:
-                stem_w[slot] = stem_block(spread, base, BLOCKS[block])
-        conv_w[...] = jnp.zeros_like(conv_w)
-        for n, block in enumerate(BLOCKS):
-            for d in range(3):
-                for q, (_, side, tap) in enumerate(block):
-                    row = d * 256 + q * 64
-                    conv_w[n, row:row + 64, side * 128:side * 128 + 128] = conv_ref[d, tap]
-        row, col = iota((192, 256), 0), iota((192, 256), 1)
-        tap_row, g = row >> 4, row & 15
-        a, d = tap_row & 3, tap_row >> 2
-        row_of = 16 * g + 4 * (d - 1) + a
-        good = (row_of == col) & ((d > 0) | ((g & 7) > 0))
-        picked[...] = jnp.where(good, 1.0, 0.0).astype(BF16)
-
     for b in range(n_blocks):
         rows = dot(picked[...], pix_ref[b * 256:b * 256 + 256, :]).astype(BF16)
         for d in range(3):
@@ -125,56 +121,22 @@
     mean = jnp.sum(summed.reshape(n_tiles, 8, C3), axis=1) * (1.0 / 64.0)
     pooled[pl.ds(pl.multiple_of(step * n_tiles, n_tiles), n_tiles), :] = mean.astype(BF16)
 
-    @pl.when(step == steps - 1)
-    def _():
-        embed = dot(pooled[...], proj_ref[...]).astype(BF16)
-        n = embed.shape[0]
-        across = jnp.broadcast_to(ids_ref[...], (n, n))
-        own = iota((n, n), 0) == iota((n, n), 1)
-        down = jnp.sum(jnp.where(own, across, 0), axis=1, keepdims=True)
-        same = (down == across) & (iota((n, n), 0) < iota((n, n), 1))
-        rank = jnp.sum(jnp.where(same, 1, 0), axis=0, keepdims=True)
-        slot = ids_ref[...] * 8 + rank
-        n_slots = out_ref.shape[0] * 8
-        placed = jnp.where(iota((n_slots, n), 0) == slot, 1.0, 0.0)
-        live = jnp.sum(placed, axis=1, keepdims=True)
-        routed = dot(placed.astype(BF16), embed)
-        out_ref[:, :, :D] = routed.reshape(n_slots // 8, 8, D).astype(BF16)
-        out_ref[:, :, D:] = jnp.broadcast_to(live, (n_slots, 128)).reshape(n_slots // 8, 8, 128).astype(BF16)
-
-
-def encode(pixels, encoder_ids, stem_weight, conv_weight, point_weight, proj_weight, n_tile, steps=4):
-    n = pixels.shape[0]
-    flat_pixels = pixels.reshape(n * 128, 384)
-    rows = n * 128 // steps
-    n_rows = rows // 16
-    stem_t = jnp.transpose(stem_weight, (0, 2, 1, 3))
-    whole = lambda shape: pl.BlockSpec(shape, lambda i: (0,) * len(shape))
-    return pl.pallas_call(
-        functools.partial(encode_kernel, steps),
-        grid=(steps,),
-        in_specs=[
-            pl.BlockSpec((rows, 384), lambda i: (i, 0)),
-            whole((1, n)),
-            whole(stem_t.shape),
-            whole(conv_weight.shape),
-            whole(point_weight.shape),
-            whole(proj_weight.shape),
-        ],
-        out_specs=whole((n_tile, 8, LINE)),
-        out_shape=jax.ShapeDtypeStruct((n_tile, 8, LINE), BF16),
-        scratch_shapes=[
-            pltpu.VMEM((64, 64), F32),
-            pltpu.VMEM((4, 256, 256), BF16),
-            pltpu.VMEM((3, 768, 256), BF16),
-            pltpu.VMEM((192, 256), BF16),
-            pltpu.VMEM((3, 6 * n_rows, 256), BF16),
-            pltpu.VMEM((3, 2 * n_rows, 768), BF16),
-            pltpu.VMEM((8 * n_rows, 128), BF16),
-            pltpu.VMEM((n, C3), BF16),
-        ],
-        name="encode_tiles",
-    )(flat_pixels, encoder_ids.reshape(1, n), stem_t, conv_weight, point_weight, proj_weight)
+
+def route(ids_ref, proj_ref, pooled, sent):
+    embed = dot(pooled[...], proj_ref[...]).astype(BF16)
+    n = embed.shape[0]
+    across = jnp.broadcast_to(ids_ref[...], (n, n))
+    own = iota((n, n), 0) == iota((n, n), 1)
+    down = jnp.sum(jnp.where(own, across, 0), axis=1, keepdims=True)
+    same = (down == across) & (iota((n, n), 0) < iota((n, n), 1))
+    rank = jnp.sum(jnp.where(same, 1, 0), axis=0, keepdims=True)
+    slot = ids_ref[...] * 8 + rank
+    n_slots = sent.shape[0] * 8
+    placed = jnp.where(iota((n_slots, n), 0) == slot, 1.0, 0.0)
+    live = jnp.sum(placed, axis=1, keepdims=True)
+    routed = dot(placed.astype(BF16), embed)
+    sent[:, :, :D] = routed.reshape(n_slots // 8, 8, D).astype(BF16)
+    sent[:, :, D:] = jnp.broadcast_to(live, (n_slots, 128)).reshape(n_slots // 8, 8, 128).astype(BF16)
 
 
 def spread_rows(n, minor):
@@ -187,21 +149,8 @@
     return lax.dot_general(a, b, (((1,), (1,)), ((), ())), preferred_element_type=F32)
 
 
-def layer_kernel(n_tile, n_seq, sent, qkv_hbm, out_hbm, o_ref, got, qkv_w, out_w, kv_send, kv_all, context,
-                 weight_sem, own_sem, send_sem, recv_sem, kv_send_sem, kv_recv_sem):
-    t, s = lax.axis_index("tile"), lax.axis_index("seq")
-    load_qkv = pltpu.make_async_copy(qkv_hbm, qkv_w, weight_sem.at[0])
-    load_out = pltpu.make_async_copy(out_hbm, out_w, weight_sem.at[1])
-    load_qkv.start()
-    load_out.start()
-    barrier = pltpu.get_barrier_semaphore()
-    for k in range(1, n_tile):
-        pl.semaphore_signal(barrier, inc=1, device_id={"tile": lax.rem(t + k, n_tile)}, device_id_type=MESH)
-    for k in range(1, n_seq):
-        pl.semaphore_signal(barrier, inc=1, device_id={"seq": lax.rem(s + k, n_seq)}, device_id_type=MESH)
-    keep = pltpu.make_async_copy(sent.at[t], got.at[t], own_sem)
-    keep.start()
-    pl.semaphore_wait(barrier, n_tile + n_seq - 2)
+def layer(t, s, n_tile, n_seq, sent, load_qkv, load_out, o_ref, got, qkv_w, out_w, kv_send, kv_all, context,
+          send_sem, recv_sem, kv_send_sem, kv_recv_sem):
     moves = []
     for k in range(1, n_tile):
         peer = lax.rem(t + k, n_tile)
@@ -211,7 +160,7 @@
         moves[-1].start()
     n = n_tile * 8
     low = iota((n, 128), 1) < HEAD_SIZE
-    keep.wait()
+    got[t] = sent[t]
     for move in moves:
         move.wait()
 
@@ -301,17 +250,75 @@
         o_ref[:, lanes] = jnp.where(alive, final[:, lanes], 0.0).astype(BF16)
 
 
-def slide_layer(sent, qkv_weight, out_weight):
+def whole_kernel(steps, n_tile, n_seq, pix_ref, ids_ref, stem_ref, conv_ref, point_ref, proj_ref, qkv_hbm, out_hbm, o_ref,
+                 flat, stem_w, conv_w, picked, packed, hidden, middle, pooled, sent,
+                 got, qkv_w, out_w, kv_send, kv_all, context,
+                 weight_sem, send_sem, recv_sem, kv_send_sem, kv_recv_sem):
+    step = pl.program_id(0)
+    n_tiles = pix_ref.shape[0] // 128
+    t, s = lax.axis_index("tile"), lax.axis_index("seq")
+    load_qkv = pltpu.make_async_copy(qkv_hbm, qkv_w, weight_sem.at[0])
+    load_out = pltpu.make_async_copy(out_hbm, out_w, weight_sem.at[1])
+    barrier = pltpu.get_barrier_semaphore()
+
+    @pl.when(step == 0)
+    def _():
+        for k in range(1, n_tile):
+            pl.semaphore_signal(barrier, inc=1, device_id={"tile": lax.rem(t + k, n_tile)}, device_id_type=MESH)
+        for k in range(1, n_seq):
+            pl.semaphore_signal(barrier, inc=1, device_id={"seq": lax.rem(s + k, n_seq)}, device_id_type=MESH)
+        prepare(stem_ref, conv_ref, flat, stem_w, conv_w, picked)
+
+    encode_step(step, n_tiles, pix_ref, point_ref, stem_w, conv_w, picked, packed, hidden, middle, pooled)
+
+    @pl.when(step == steps - 1)
+    def _():
+        load_qkv.start()
+        load_out.start()
+        route(ids_ref, proj_ref, pooled, sent)
+        pl.semaphore_wait(barrier, n_tile + n_seq - 2)
+        layer(t, s, n_tile, n_seq, sent, load_qkv, load_out, o_ref, got, qkv_w, out_w, kv_send, kv_all, context,
+              send_sem, recv_sem, kv_send_sem, kv_recv_sem)
+
+
+def body(
+    pixels, encoder_ids, stem_weight, conv_weight, point_weight, proj_weight, qkv_weight, out_weight
+):
     n_tile, n_seq = lax.axis_size("tile"), lax.axis_size("seq")
+    steps = 4
+    tiles = pixels.shape[0]
+    rows = tiles * 128 // steps
+    n_rows = rows // 16
     n = n_tile * 8
+    blocks = 2 * D // 128 + 1
+    stem_t = jnp.transpose(stem_weight, (0, 2, 1, 3))
+    whole = lambda shape: pl.BlockSpec(shape, lambda i: (0,) * len(shape))
     anywhere = pl.BlockSpec(memory_space=pl.ANY)
-    blocks = 2 * D // 128 + 1
-    return pl.pallas_call(
-        functools.partial(layer_kernel, n_tile, n_seq),
-        in_specs=[anywhere] * 3,
-        out_specs=pl.BlockSpec(memory_space=pltpu.VMEM),
+    out = pl.pallas_call(
+        functools.partial(whole_kernel, steps, n_tile, n_seq),
+        grid=(steps,),
+        in_specs=[
+            pl.BlockSpec((rows, 384), lambda i: (i, 0)),
+            whole((1, tiles)),
+            whole(stem_t.shape),
+            whole(conv_weight.shape),
+            whole(point_weight.shape),
+            whole(proj_weight.shape),
+            anywhere,
+            anywhere,
+        ],
+        out_specs=whole((n, D)),
         out_shape=jax.ShapeDtypeStruct((n, D), BF16),
         scratch_shapes=[
+            pltpu.VMEM((64, 64), F32),
+            pltpu.VMEM((4, 256, 256), BF16),
+            pltpu.VMEM((3, 768, 256), BF16),
+            pltpu.VMEM((192, 256), BF16),
+            pltpu.VMEM((3, 6 * n_rows, 256), BF16),
+            pltpu.VMEM((3, 2 * n_rows, 768), BF16),
+            pltpu.VMEM((8 * n_rows, 128), BF16),
+            pltpu.VMEM((tiles, C3), BF16),
+            pltpu.VMEM((n_tile, 8, LINE), BF16),
             pltpu.VMEM((n_tile, 8, LINE), BF16),
             pltpu.VMEM(qkv_weight.shape, BF16),
             pltpu.VMEM(out_weight.shape, BF16),
@@ -319,23 +326,16 @@
             pltpu.VMEM((n_seq, blocks, n_tile, 128), BF16),
             pltpu.VMEM((n, D), BF16),
             pltpu.SemaphoreType.DMA((2,)),
-            pltpu.SemaphoreType.DMA,
             pltpu.SemaphoreType.DMA((n_tile - 1,)),
             pltpu.SemaphoreType.DMA((n_tile - 1,)),
             pltpu.SemaphoreType.DMA((n_seq - 1,)),
             pltpu.SemaphoreType.DMA((n_seq - 1,)),
         ],
         compiler_params=pltpu.CompilerParams(collective_id=0, has_side_effects=True),
-        name="slide_layer",
-    )(sent, qkv_weight, out_weight)
-
-
-def body(
-    pixels, encoder_ids, stem_weight, conv_weight, point_weight, proj_weight, qkv_weight, out_weight
-):
-    n_tile = lax.axis_size("tile")
-    sent = encode(pixels, encoder_ids, stem_weight, conv_weight, point_weight, proj_weight, n_tile)
-    return slide_layer(sent, qkv_weight, out_weight)[None]
+        name="tiles_to_slide",
+    )(pixels.reshape(tiles * 128, 384), encoder_ids.reshape(1, tiles), stem_t, conv_weight, point_weight, proj_weight,
+      qkv_weight, out_weight)
+    return out[None]
 
 
 def solution(mesh):

time: 36.5 us -> 33.7 us (0.923)
  Pallas kernels: 34.7 us -> 31.9 us
    pallas_call x2 -> x1, Pallas kernels: 34.7 us -> 31.9 us  [body(): pl.pallas_call(functools.partial(whole_kernel, steps, n_tile, n_seq), gri...]
where the time goes in v3:
time: 33.7 us; the launch traced here: 33.5 us
  Pallas kernels  31.9 us (95%)
  local copies, waits for them, and re-layouts  1.62 us (5%)
    pallas_call x1, Pallas kernels, body(): pl.pallas_call(functools.partial(whole_kernel, steps, n_tile, n_seq), gri...  31.9 us
    unnamed x1, local copies, waits for them, and re-layouts  1.62 us

profile of v3, /device:TPU:1, one launch (start us, length us, event | category | flops | bytes accessed | tf_op | source)
XLA Modules:
  0.0 33.5 jit_solution(5165605689054404074)
XLA Ops:
  0.0 31.9 %tiles_to_slide.1 = bf16[128,768]{1,0:T(8,128)(2,1)} custom-call(bf16[8192,384]{1,0:T(8,128)(2,1)} %bitcast.4, s32[1,64]{1,0:T(1,128)} %bitcast.7, bf16[4,3,4,64]{3,2,1,0:T(4,128)(2,1)} %bitcast.6, bf16[3,3,64,128]{3,2,1,0:T(8,128)(2,1)} %conv_ref.1, bf16[128,256]{1,0:T(8,128)(2,1)} %point_ref.1, bf16[256,768]{1,0:T(8,128)(2,1)} %proj_ref.1, ...), custom_call_target="tpu_custom_call" | custom-call | tf_op jit(solution)/shard_map/tiles_to_slide/pallas_call | solution.py:297
  31.9 1.6 %copy.10 = bf16[1,128,768]{2,1,0:T(8,128)(2,1)} copy(bf16[1,128,768]{2,1,0:T(8,128)(2,1)} %bitcast.5) | data formatting | bytes 393216

commit v4 on v3

v4 whole, which is shorter than its diff:
```python
import functools
import math
import jax
import jax.numpy as jnp
from jax import lax
from jax.sharding import PartitionSpec as P
from jax.experimental import pallas as pl
from jax.experimental.pallas import tpu as pltpu

D = 768
C1, C2, C3 = 64, 128, 256
GROUP = 16
LINE = D + 128
HEAD_SIZE = 64
F32, BF16 = jnp.float32, jnp.bfloat16
MESH = pl.DeviceIdType.MESH

BLOCKS = (
    ((0, 0, 1), (1, 0, 2), (3, 1, 0), (4, 1, 1)),
    ((5, 0, 2), (7, 1, 0), (8, 1, 1), (9, 1, 2)),
    ((11, 0, 0), (12, 0, 1), (13, 0, 2), (15, 1, 0)),
)


def iota(shape, dim):
    return lax.broadcasted_iota(jnp.int32, shape, dim)


def dot(a, b):
    return jnp.dot(a, b, preferred_element_type=F32)


def stem_spread(flat_ref, base):
    taps = iota((64, 64), 1)
    lane = iota((64, 64), 0) + base
    lane = lane - 12 * jnp.floor((lane.astype(F32) + 0.5) * (1.0 / 12.0)).astype(jnp.int32)
    colour, column = (taps & 15) >> 2, taps & 3
    hit = jnp.where((colour < 3) & (lane == 3 * column + colour), 1.0, 0.0)
    chosen = jnp.concatenate([jnp.where((taps >> 4) == a, hit, 0.0) for a in range(4)], axis=0)
    tiled = jnp.where((iota((64, 256), 1) & 63) == iota((64, 256), 0), 1.0, 0.0).astype(BF16)
    wide = dot(flat_ref[...].astype(BF16), tiled).astype(BF16)
    return dot(chosen.astype(BF16), wide)


def stem_block(spread, base, block):
    quarter = iota((1, 256), 1) >> 6
    first = jnp.zeros((1, 256), jnp.int32)
    for q, (column, _, _) in enumerate(block):
        first = jnp.where(quarter == q, 12 * column, first)
    lane = iota((64, 256), 0) + base - first
    inside = (lane >= 0) & (lane < 12)
    return jnp.concatenate([jnp.where(inside, spread[a * 64:(a + 1) * 64], 0.0) for a in range(4)], axis=0).astype(BF16)


def prepare(stem_ref, conv_ref, flat, stem_w, conv_w, picked):
    flat[...] = jnp.zeros_like(flat)
    for a in range(4):
        for c in range(3):
            flat[a * 16 + c * 4:a * 16 + c * 4 + 4, :] = stem_ref[a, c].astype(F32)
    for base, uses in ((0, ((0, 0), (1, 1))), (64, ((2, 1),)), (128, ((3, 2),))):
        spread = stem_spread(flat, base)
        for slot, block in uses:
            stem_w[slot] = stem_block(spread, base, BLOCKS[block])
    none = jnp.zeros((64, 128), BF16)
    for n, block in enumerate(BLOCKS):
        for d in range(3):
            for q, (_, side, tap) in enumerate(block):
                row = d * 256 + q * 64
                conv_w[n, row:row + 64, side * 128:side * 128 + 128] = conv_ref[d, tap]
                conv_w[n, row:row + 64, (1 - side) * 128:(1 - side) * 128 + 128] = none
    row, col = iota((192, 256), 0), iota((192, 256), 1)
    tap_row, g = row >> 4, row & 15
    a, d = tap_row & 3, tap_row >> 2
    row_of = 16 * g + 4 * (d - 1) + a
    good = (row_of == col) & ((d > 0) | ((g & 7) > 0))
    picked[...] = jnp.where(good, 1.0, 0.0).astype(BF16)


def regroup(first_row, n_tiles, pix, picked, packed):
    n_blocks, n_rows = n_tiles // 2, n_tiles * 8
    low = iota((16, 128), 1) < 64
    for b in range(n_blocks):
        rows = dot(picked[...], pix[first_row + b * 256:first_row + b * 256 + 256, :])
        for d in range(3):
            for pair in range(2):
                first = (d * 4 + pair * 2) * 16
                for c in range(3):
                    lanes = slice(c * 128, (c + 1) * 128)
                    p0, p1 = rows[first:first + 16, lanes], rows[first + 16:first + 32, lanes]
                    r0, r1 = pltpu.roll(p0, 64, 1), pltpu.roll(p1, 64, 1)
                    for half, both in enumerate((jnp.where(low, p0, r1), jnp.where(low, r0, p1))):
                        h, u = divmod(2 * c + half, 3)
                        at = (h * 3 + d) * n_rows + b * 16
                        packed[u, at:at + 16, pair * 128:pair * 128 + 128] = both.astype(BF16)


def convolve(chunk, n_tiles, point_ref, stem_w, conv_w, packed, hidden, middle, pooled):
    n_rows = n_tiles * 8
    for n, terms in enumerate((((0, 0),), ((0, 1), (1, 2)), ((2, 3),))):
        total = dot(packed[terms[0][0]], stem_w[terms[0][1]])
        for u, w in terms[1:]:
            total = total + dot(packed[u], stem_w[w])
        total = jnp.maximum(total, 0.0).astype(BF16)
        for h in range(2):
            for d in range(3):
                hidden[n, h * n_rows:(h + 1) * n_rows, d * 256:(d + 1) * 256] = (
                    total[(h * 3 + d) * n_rows:(h * 3 + d + 1) * n_rows])
    left = dot(hidden[0], conv_w[0])
    mid = dot(hidden[1], conv_w[1])
    right = dot(hidden[2], conv_w[2])
    for h in range(2):
        rows = slice(h * n_rows, (h + 1) * n_rows)
        first = left[rows, :128]
        if h == 1:
            first = first + right[:n_rows, 128:]
        cols = (first, left[rows, 128:] + mid[rows, :128], mid[rows, 128:], right[rows, :128])
        for j, col in enumerate(cols):
            at = (h * 4 + j) * n_rows
            middle[at:at + n_rows, :] = jnp.maximum(col, 0.0).astype(BF16)
    point = jnp.maximum(dot(middle[...], point_ref[...]), 0.0)
    summed = point[:n_rows]
    for j in range(1, 8):
        summed = summed + point[j * n_rows:(j + 1) * n_rows]
    mean = jnp.sum(summed.reshape(n_tiles, 8, C3), axis=1) * (1.0 / 64.0)
    pooled[chunk * n_tiles:(chunk + 1) * n_tiles, :] = mean.astype(BF16)


def route(ids_ref, proj_ref, pooled, sent):
    embed = dot(pooled[...], proj_ref[...]).astype(BF16)
    n = embed.shape[0]
    across = jnp.broadcast_to(ids_ref[...], (n, n))
    own = iota((n, n), 0) == iota((n, n), 1)
    down = jnp.sum(jnp.where(own, across, 0), axis=1, keepdims=True)
    same = (down == across) & (iota((n, n), 0) < iota((n, n), 1))
    rank = jnp.sum(jnp.where(same, 1, 0), axis=0, keepdims=True)
    slot = ids_ref[...] * 8 + rank
    n_slots = sent.shape[0] * 8
    placed = jnp.where(iota((n_slots, n), 0) == slot, 1.0, 0.0)
    live = jnp.sum(placed, axis=1, keepdims=True)
    routed = dot(placed.astype(BF16), embed)
    sent[:, :, :D] = routed.reshape(n_slots // 8, 8, D).astype(BF16)
    sent[:, :, D:] = jnp.broadcast_to(live, (n_slots, 128)).reshape(n_slots // 8, 8, 128).astype(BF16)


def spread_rows(n, minor):
    row, col = iota((n, n), 0), iota((n, n), 1)
    shift = minor.bit_length() - 1
    return jnp.where(col == (row & (minor - 1)) * (n // minor) + (row >> shift), 1.0, 0.0).astype(BF16)


def dot_t(a, b):
    return lax.dot_general(a, b, (((1,), (1,)), ((), ())), preferred_element_type=F32)


def torus_order(n):
    side = math.isqrt(n)
    hops = lambda k: sum(min(d, side - d) for d in divmod(k, side))
    return sorted(range(1, n), key=lambda k: (-hops(k), k))


def torus_peer(t, k, n):
    side = math.isqrt(n)
    return lax.rem(t // side + k // side, side) * side + lax.rem(lax.rem(t, side) + k % side, side)


def layer(t, s, n_tile, n_seq, sent, load_qkv, load_out, o_ref, got, qkv_w, out_w, kv_send, kv_all, context,
          send_sem, recv_sem, kv_send_sem, kv_recv_sem):
    moves = []
    for k in torus_order(n_tile):
        peer = torus_peer(t, k, n_tile)
        moves.append(pltpu.make_async_remote_copy(
            src_ref=sent.at[peer], dst_ref=got.at[t], send_sem=send_sem.at[k - 1], recv_sem=recv_sem.at[k - 1],
            device_id={"tile": peer}, device_id_type=MESH))
        moves[-1].start()
    n = n_tile * 8
    low = iota((n, 128), 1) < HEAD_SIZE
    got[t] = sent[t]
    for move in moves:
        move.wait()

    natural = got[...].astype(F32).reshape(n, LINE)
    rows = dot(spread_rows(n, n_tile), natural.astype(BF16))
    live = rows[:, D:]
    rows = rows[:, :D]
    power = jnp.mean(rows * rows, axis=-1, keepdims=True)
    normed = (rows * lax.rsqrt(power + 1e-06)).astype(BF16)
    load_qkv.wait()
    pairs = D // 128
    kv = dot(normed, qkv_w[:, D:]).astype(BF16)
    low16 = low[:n_tile]

    def offsets(m):
        a = (2 * m) % n_seq
        b = (2 * m + 1) % n_seq
        return slice(a * n_tile, (a + 1) * n_tile), slice(b * n_tile, (b + 1) * n_tile)

    for m in range(2 * pairs):
        chunk = kv[:, m * 128:(m + 1) * 128]
        first, second = offsets(m % pairs)
        kv_send[m] = jnp.where(low16, chunk[first], chunk[second])
    flags = jnp.zeros((n_tile, 128), F32)
    for r in range(n_seq):
        flags = jnp.where(iota((n_tile, 128), 1) == r, live[r * n_tile:(r + 1) * n_tile], flags)
    kv_send[2 * pairs] = flags.astype(BF16)
    twin = s + 1 - 2 * lax.rem(s, 2)
    far_offsets = sorted(range(2, n_seq, 2), key=lambda k: (-min(k, n_seq - k), k))
    kv_moves, forwards = {}, {}
    for k in far_offsets:
        kv_moves[k] = pltpu.make_async_remote_copy(
            src_ref=kv_send, dst_ref=kv_all.at[s], send_sem=kv_send_sem.at[k - 1], recv_sem=kv_recv_sem.at[k - 1],
            device_id={"seq": lax.rem(s + k, n_seq)}, device_id_type=MESH)
        kv_moves[k].start()
    to_twin = pltpu.make_async_remote_copy(
        src_ref=kv_send, dst_ref=kv_all.at[s], send_sem=kv_send_sem.at[0], recv_sem=kv_recv_sem.at[0],
        device_id={"seq": twin}, device_id_type=MESH)
    to_twin.start()
    kv_all[s] = kv_send[...]

    def hand_on(k):
        kv_moves[k].wait_recv()
        source = lax.rem(s + n_seq - k, n_seq)
        forwards[k] = pltpu.make_async_remote_copy(
            src_ref=kv_all.at[source], dst_ref=kv_all.at[source], send_sem=kv_send_sem.at[k], recv_sem=kv_recv_sem.at[k],
            device_id={"seq": twin}, device_id_type=MESH)
        forwards[k].start()

    query = (dot(normed, qkv_w[:, :D]).astype(BF16) * 0.125).astype(BF16)
    live_across = jnp.transpose(live)
    own = iota((n, n), 0) == iota((n, n), 1)
    bias = jnp.where((live_across > 0.5) | own, 0.0, -1e30)
    bias = jnp.concatenate([bias, bias], axis=0)
    none = jnp.zeros((n, 128), BF16)
    kept = []
    for m in range(pairs):
        lanes = slice(m * 128, (m + 1) * 128)
        q = query[:, lanes]
        q = jnp.concatenate([jnp.where(low, q, none), jnp.where(low, none, q)], axis=0)
        score = dot_t(q, kv[:, lanes]) + bias
        top = jnp.max(score, axis=-1, keepdims=True)
        weight = jnp.exp(score - top)
        total = jnp.sum(weight, axis=-1, keepdims=True)
        summed = dot(weight.astype(BF16), kv[:, D + m * 128:D + (m + 1) * 128])
        result = summed / total
        context[:, lanes] = jnp.where(low, result[:n], result[n:]).astype(BF16)
        first, second = offsets(m)
        second = slice(n + second.start, n + second.stop)
        if m == pairs - 3:
            for k in far_offsets[1:]:
                hand_on(k)
        kept.append([jnp.concatenate([x[first], x[second]], axis=0) for x in (q, top, total, summed)])

    hand_on(far_offsets[0])
    to_twin.wait()
    for k in far_offsets:
        kv_moves[k].wait_send()
    for k in far_offsets:
        forwards[k].wait()
    there = kv_all[:, 2 * pairs].reshape(n, 128)
    pick = jnp.where(iota((n_tile, 128), 0) == iota((n_tile, 128), 1), 1.0, 0.0).astype(BF16)
    far_bias = jnp.where(dot_t(pick, there) > 0.5, 0.0, -1e30)
    scores = []
    for m in range(pairs):
        for half in offsets(m):
            a = half.start // n_tile
            scores.append(jnp.broadcast_to(far_bias[a:a + 1], (n_tile, 128)))
    join = lambda parts: jnp.concatenate(parts, axis=0)
    q, top, total, summed = [join(parts) for parts in zip(*kept)]
    size = 2 * n_tile
    block = lambda x, m: x[m * size:(m + 1) * size]
    score = join([dot_t(block(q, m), kv_all[:, m].reshape(n, 128)) for m in range(pairs)]) + join(scores)
    new_top = jnp.maximum(top, jnp.max(score, axis=-1, keepdims=True))
    weight = jnp.exp(score - new_top)
    scale = jnp.exp(top - new_top)
    total = total * scale + jnp.sum(weight, axis=-1, keepdims=True)
    weight = weight.astype(BF16)
    more = join([dot(block(weight, m), kv_all[:, pairs + m].reshape(n, 128)) for m in range(pairs)])
    result = ((summed * scale + more) / total).astype(BF16)
    for m in range(pairs):
        lanes = slice(m * 128, (m + 1) * 128)
        first, second = offsets(m)
        mine = block(result, m)
        context[first, lanes] = jnp.where(low16, mine[:n_tile], context[first, lanes])
        context[second, lanes] = jnp.where(low16, context[second, lanes], mine[n_tile:])

    back = dot(spread_rows(n, n_seq), context[...]).astype(BF16)
    load_out.wait()
    final = dot(back, out_w[...])
    alive = natural[:, D:] > 0.5
    for m in range(pairs):
        lanes = slice(m * 128, (m + 1) * 128)
        o_ref[:, lanes] = jnp.where(alive, final[:, lanes], 0.0).astype(BF16)


def whole_kernel(chunks, n_tile, n_seq, pix_hbm, ids_hbm, stem_hbm, conv_hbm, point_hbm, proj_hbm, qkv_hbm, out_hbm, o_ref,
                 pix, ids, stem, conv, point, proj, qkv_w, out_w,
                 flat, stem_w, conv_w, picked, packed_a, packed_b, hidden, middle, pooled, sent,
                 got, kv_send, kv_all, context,
                 pix_sem, weight_sem, send_sem, recv_sem, kv_send_sem, kv_recv_sem):
    rows = pix.shape[0] // chunks
    n_tiles = rows // 128
    t, s = lax.axis_index("tile"), lax.axis_index("seq")
    part = lambda ref, i: ref.at[pl.ds(i * rows, rows)]
    load_pix = [pltpu.make_async_copy(part(pix_hbm, i), part(pix, i), pix_sem.at[i]) for i in range(chunks)]
    pairs = ((stem_hbm, stem), (conv_hbm, conv), (point_hbm, point), (ids_hbm, ids), (proj_hbm, proj),
             (qkv_hbm, qkv_w), (out_hbm, out_w))
    load_stem, load_conv, load_point, load_ids, load_proj, load_qkv, load_out = [
        pltpu.make_async_copy(a, b, weight_sem.at[i]) for i, (a, b) in enumerate(pairs)]
    for load in (load_stem, load_conv, load_pix[0], load_point, *load_pix[1:], load_ids, load_proj, load_qkv, load_out):
        load.start()
    barrier = pltpu.get_barrier_semaphore()
    for k in range(1, n_tile):
        pl.semaphore_signal(barrier, inc=1, device_id={"tile": lax.rem(t + k, n_tile)}, device_id_type=MESH)
    for k in range(1, n_seq):
        pl.semaphore_signal(barrier, inc=1, device_id={"seq": lax.rem(s + k, n_seq)}, device_id_type=MESH)
    load_stem.wait()
    load_conv.wait()
    prepare(stem, conv, flat, stem_w, conv_w, picked)
    packed = (packed_a, packed_b)
    for i in range(chunks + 1):
        if i < chunks:
            load_pix[i].wait()
            if i == 0:
                load_point.wait()
            regroup(i * rows, n_tiles, pix, picked, packed[i % 2])
        if i > 0:
            convolve(i - 1, n_tiles, point, stem_w, conv_w, packed[(i - 1) % 2], hidden, middle, pooled)
    load_ids.wait()
    load_proj.wait()
    route(ids, proj, pooled, sent)
    pl.semaphore_wait(barrier, n_tile + n_seq - 2)
    layer(t, s, n_tile, n_seq, sent, load_qkv, load_out, o_ref, got, qkv_w, out_w, kv_send, kv_all, context,
          send_sem, recv_sem, kv_send_sem, kv_recv_sem)


def body(
    pixels, encoder_ids, stem_weight, conv_weight, point_weight, proj_weight, qkv_weight, out_weight
):
    n_tile, n_seq = lax.axis_size("tile"), lax.axis_size("seq")
    chunks = 4
    tiles = pixels.shape[0]
    n_rows = tiles // chunks * 8
    n = n_tile * 8
    blocks = 2 * D // 128 + 1
    operands = (pixels.reshape(tiles * 128, 384), encoder_ids.reshape(1, tiles), jnp.transpose(stem_weight, (0, 2, 1, 3)),
                conv_weight, point_weight, proj_weight, qkv_weight, out_weight)
    out = pl.pallas_call(
        functools.partial(whole_kernel, chunks, n_tile, n_seq),
        in_specs=[pl.BlockSpec(memory_space=pl.ANY)] * len(operands),
        out_specs=pl.BlockSpec(memory_space=pltpu.VMEM),
        out_shape=jax.ShapeDtypeStruct((n, D), BF16),
        scratch_shapes=[pltpu.VMEM(x.shape, x.dtype) for x in operands] + [
            pltpu.VMEM((64, 64), F32),
            pltpu.VMEM((4, 256, 256), BF16),
            pltpu.VMEM((3, 768, 256), BF16),
            pltpu.VMEM((192, 256), BF16),
            pltpu.VMEM((3, 6 * n_rows, 256), BF16),
            pltpu.VMEM((3, 6 * n_rows, 256), BF16),
            pltpu.VMEM((3, 2 * n_rows, 768), BF16),
            pltpu.VMEM((8 * n_rows, 128), BF16),
            pltpu.VMEM((tiles, C3), BF16),
            pltpu.VMEM((n_tile, 8, LINE), BF16),
            pltpu.VMEM((n_tile, 8, LINE), BF16),
            pltpu.VMEM((blocks, n_tile, 128), BF16),
            pltpu.VMEM((n_seq, blocks, n_tile, 128), BF16),
            pltpu.VMEM((n, D), BF16),
            pltpu.SemaphoreType.DMA((chunks,)),
            pltpu.SemaphoreType.DMA((len(operands) - 1,)),
            pltpu.SemaphoreType.DMA((n_tile - 1,)),
            pltpu.SemaphoreType.DMA((n_tile - 1,)),
            pltpu.SemaphoreType.DMA((n_seq - 1,)),
            pltpu.SemaphoreType.DMA((n_seq - 1,)),
        ],
        compiler_params=pltpu.CompilerParams(collective_id=0, has_side_effects=True),
        name="tiles_to_slide",
    )(*operands)
    return out[None]


def solution(mesh):
    return jax.shard_map(
        body,
        mesh=mesh,
        in_specs=(
            P(("tile", "seq"), None, None),
            P(("tile", "seq"), None),
            P(),
            P(),
            P(),
            P(),
            P(),
            P(),
        ),
        out_specs=P("tile", "seq", None),
        check_vma=False,
    )
```

time: 33.7 us -> 30.8 us (0.914)
  Pallas kernels: 31.9 us -> 29 us
    pallas_call x1, Pallas kernels: 31.9 us -> 29 us  [body(): pl.pallas_call(functools.partial(whole_kernel, chunks, n_tile, n_seq), in...]
where the time goes in v4:
time: 30.8 us; the launch traced here: 30.7 us
  Pallas kernels  29 us (94%)
  local copies, waits for them, and re-layouts  1.62 us (5%)
    pallas_call x1, Pallas kernels, body(): pl.pallas_call(functools.partial(whole_kernel, chunks, n_tile, n_seq), in...  29 us
    unnamed x1, local copies, waits for them, and re-layouts  1.62 us

profile of v4, /device:TPU:1, one launch (start us, length us, event | category | flops | bytes accessed | tf_op | source)
XLA Modules:
  0.0 30.7 jit_solution(4999287384748081973)
XLA Ops:
  0.0 29.0 %tiles_to_slide.1 = bf16[128,768]{1,0:T(8,128)(2,1)} custom-call(bf16[8192,384]{1,0:T(8,128)(2,1)} %bitcast.4, s32[1,64]{1,0:T(1,128)} %bitcast.7, bf16[4,3,4,64]{3,2,1,0:T(4,128)(2,1)} %bitcast.6, bf16[3,3,64,128]{3,2,1,0:T(8,128)(2,1)} %conv_hbm.1, bf16[128,256]{1,0:T(8,128)(2,1)} %point_hbm.1, bf16[256,768]{1,0:T(8,128)(2,1)} %proj_hbm.1, ...), custom_call_target="tpu_custom_call" | custom-call | tf_op jit(solution)/shard_map/tiles_to_slide/pallas_call | solution.py:346
  29.1 1.6 %copy.10 = bf16[1,128,768]{2,1,0:T(8,128)(2,1)} copy(bf16[1,128,768]{2,1,0:T(8,128)(2,1)} %bitcast.5) | data formatting | bytes 393216
